TPU v7x, 256 devices: a whole 4x4x8 slice. The times are simulated.
256 devices in a mesh: feat: 16 (over z, x_hi), tok: 16 (over x_lo, y, core).
Axes of the slice: x: 4 (x_hi: 2, x_lo: 2; x = x_hi * 2 + x_lo), y: 4, z: 8, core: 2. Of those that a mesh axis runs over, the one named last changes fastest.
Arguments:
- activations: bfloat16 [8192, 32768], P('tok', 'feat'), may hold values from -48 to 48
- pattern: int32 [192, 2], replicated, may hold values from 0 to 63, as said below
- block_slot: int32 [192], replicated, may hold values from 0 to 191
Outputs:
- gram_blocks: float32 [512, 192, 512], P('tok', 'feat')
Inputs may be any that keep to these rules, and one draw needn't show every extreme that they name: `pattern`: block_slot is a permutation of the slots. The row block of the listed block stored at slot s lies in the panel of feat index s // 12 (blocks k * 4 to k * 4 + 3 for index k). Among the column blocks of the 12 slots of one feat index, at most 1 lie in any one index's panel, and exactly 1 in some.
All inputs are finite; a program needn't handle non-finite values.
Results may differ from a plain program's by a relative error of at most 0.0003.
Values may be sent and summed in bfloat16 or wider, within the bound.
A program may use at most 128 MiB of HBM per device.

v0:
```python
import jax
import jax.numpy as jnp
from jax import lax
from jax.sharding import PartitionSpec as P

BLK = 512


def body(activations, pattern, block_slot):
    tok_rows, width = activations.shape
    feat_count = lax.axis_size("feat")
    tok_count = lax.axis_size("tok")
    my_index = lax.axis_index("feat")
    panel_blocks = width // BLK
    list_length = pattern.shape[0]
    per_device = list_length // feat_count
    capacity = (per_device + feat_count - 1) // feat_count
    scale = 1.0 / (tok_rows * tok_count)
    ordered = jnp.zeros_like(pattern).at[block_slot].set(pattern)
    pairs = ordered.reshape(feat_count, per_device, 2)
    holder = pairs[:, :, 1] // panel_blocks
    local_column = pairs[:, :, 1] % panel_blocks
    positions = jnp.arange(per_device)
    same_holder = holder[:, :, None] == holder[:, None, :]
    before = positions[None, None, :] < positions[None, :, None]
    rank = jnp.sum((same_holder & before).astype(jnp.int32), axis=2)
    blocks_local = activations.reshape(tok_rows, panel_blocks, BLK)
    slot_range = jnp.arange(capacity)
    my_holder = lax.dynamic_index_in_dim(holder, my_index, 0, keepdims=False)
    my_rank = lax.dynamic_index_in_dim(rank, my_index, 0, keepdims=False)
    my_pairs = lax.dynamic_index_in_dim(pairs, my_index, 0, keepdims=False)
    everyone = jnp.arange(feat_count)
    dest_holder = holder[everyone]
    dest_rank = rank[everyone]
    dest_column = local_column[everyone]
    match = (dest_holder[:, None, :] == my_index) & (
        dest_rank[:, None, :] == slot_range[None, :, None]
    )
    picked = jnp.sum(jnp.where(match, dest_column[:, None, :], 0), axis=2).reshape(-1)
    received = lax.all_to_all(
        jnp.take(blocks_local, picked, axis=1), "feat", split_axis=1, concat_axis=1, tiled=True
    )
    lookup = my_holder * capacity + my_rank
    row_blocks = jnp.take(blocks_local, my_pairs[:, 0] % panel_blocks, axis=1)
    column_blocks = jnp.take(received, lookup, axis=1)
    return lax.psum_scatter(
        jnp.einsum("tki,tkj->ikj", row_blocks, column_blocks, preferred_element_type=jnp.float32)
        * scale,
        "tok",
        scatter_dimension=0,
        tiled=True,
    )


def solution(mesh):
    placed = (P("tok", "feat"), P(), P())
    return jax.shard_map(
        body, mesh=mesh, in_specs=placed, out_specs=P("tok", "feat", None), check_vma=False
    )
```

profile of v0, /device:TPU:69, one launch (start us, length us, event | category | flops | bytes accessed | tf_op | source)
XLA Modules:
  0.0 381.1 jit_solution(17623080956428196520)
XLA Ops:
  6.5 0.7 compare_select_fusion
  7.2 0.8 copy.25
  8.0 1.0 scatter_custom_fusion
  9.1 0.1 copy.26
  9.2 0.1 reshape.116
  9.3 0.1 copy.27
  9.4 0.4 convert_reduce_fusion
  9.8 0.1 copy.28
  9.9 0.6 gather_fusion
  10.4 0.6 gather_fusion.2
  11.0 0.6 gather_fusion.1
  11.5 0.1 select_reduce_fusion
  11.7 3.9 %copy.30 = bf16[512,2048]{0,1:T(8,128)(2,1)} copy(bf16[512,2048]{1,0:T(8,128)(2,1)} %param.3) | data formatting | bytes 4194304 | tf_op args[0]
  15.6 2.8 copy.31
  18.4 4.7 %gather_fusion.3 = bf16[16,512,512]{2,1,0:T(8,128)(2,1)} fusion(bf16[512,4,512]{2,0,1:T(8,128)(2,1)S(1)} %copy.31, s32[1024]{0:T(1024)S(1)} %pad_clamp_fusion.2), kind=kCustom, calls=%fused_computation.3 | custom fusion | bytes 16777280 | tf_op jit(solution)/shard_map/jit(_take)/gather | solution.py:41
  23.1 7.5 %select_bitcast_fusion = bf16[512,16,512]{2,0,1:T(8,128)(2,1)} fusion(bf16[16,512,512]{2,1,0:T(8,128)(2,1)} %gather_fusion.3, pred[16]{0:T(512)(128)(4,1)S(1)} %compare_and_fusion), kind=kLoop, calls=%fused_computation.8 | loop fusion | flops 4194304 | bytes 16777232 | tf_op jit(solution)/shard_map/jit(_take)/select_n | solution.py:41
  30.6 10.0 %all-to-all-start = ((bf16[512,16,512]{2,0,1:T(8,128)(2,1)}), bf16[512,16,512]{2,0,1:T(8,128)(2,1)}, u32[]{:S(2)}, u32[]{:S(2)}) async-start(bf16[512,16,512]{2,0,1:T(8,128)(2,1)} %select_bitcast_fusion), calls=%async_computation | async-start | bytes 16777216 | tf_op jit(solution)/shard_map/all_to_all | solution.py:40
  40.6 4.1 %gather_fusion.5 = bf16[12,512,512]{2,1,0:T(8,128)(2,1)} fusion(bf16[512,4,512]{2,0,1:T(8,128)(2,1)S(1)} %copy.31, s32[1024]{0:T(1024)S(1)} %pad_clamp_fusion), kind=kCustom, calls=%fused_computation.5 | custom fusion | bytes 12582960 | tf_op jit(solution)/shard_map/jit(_take)/gather | solution.py:44
  44.8 190.0 %all-to-all-done = bf16[512,16,512]{2,0,1:T(8,128)(2,1)} async-done(((bf16[512,16,512]{2,0,1:T(8,128)(2,1)}), bf16[512,16,512]{2,0,1:T(8,128)(2,1)}, u32[]{:S(2)}, u32[]{:S(2)}) %all-to-all-start) | async-done | bytes 8388640 | tf_op jit(solution)/shard_map/all_to_all | solution.py:40
  234.8 7.6 %gather_fusion.4 = bf16[12,512,512]{2,1,0:T(8,128)(2,1)} fusion(bf16[512,16,512]{2,0,1:T(8,128)(2,1)} %all-to-all-done, s32[1024]{0:T(1024)S(1)} %pad_clamp_fusion.1), kind=kCustom, calls=%fused_computation.4 | custom fusion | bytes 12582960 | tf_op jit(solution)/shard_map/jit(_take)/gather | solution.py:45
  242.5 12.8 %multiply_bitcast_fusion = f32[512,12,512]{0,2,1:T(8,128)} fusion(bf16[12,512,512]{2,1,0:T(8,128)(2,1)} %gather_fusion.5, pred[12]{0:T(512)(128)(4,1)S(1)} %get-tuple-element.9, bf16[12,512,512]{2,1,0:T(8,128)(2,1)} %gather_fusion.4, pred[12]{0:T(512)(128)(4,1)S(1)} %get-tuple-element.5), kind=kOutput, calls=%fused_computation.7 | convolution fusion | flops 3230662656 | bytes 25165848 | tf_op jit(solution)/shard_map/tki,tkj->ikj/dot_general | solution.py:47
  255.3 18.5 %copy.34 = f32[512,12,512]{2,1,0:T(8,128)} copy(f32[512,12,512]{0,2,1:T(8,128)} %multiply_bitcast_fusion) | data formatting | bytes 25165824 | tf_op jit(solution)/shard_map/mul | solution.py:47
  273.7 97.9 %reduce-scatter.2.cloned.1.call-done = f32[32,12,512]{2,1,0:T(8,128)} async-done(((f32[512,12,512]{2,1,0:T(8,128)}), f32[32,12,512]{2,1,0:T(8,128)}) %reduce-scatter.2.cloned.1.call-update) | async-done | bytes 786448 | tf_op jit(solution)/shard_map/reduce_scatter | solution.py:46
  371.7 2.6 copy.35
  (17 shorter events, 0.2 us)
Async XLA Ops:
  30.6 204.3 %all-to-all-start = ((bf16[512,16,512]{2,0,1:T(8,128)(2,1)}), bf16[512,16,512]{2,0,1:T(8,128)(2,1)}, u32[]{:S(2)}, u32[]{:S(2)}) async-start(bf16[512,16,512]{2,0,1:T(8,128)(2,1)} %select_bitcast_fusion), calls=%async_computation | async-start | bytes 16777216 | tf_op jit(solution)/shard_map/all_to_all | solution.py:40
  40.6 331.1 %reduce-scatter.2.cloned.1.call-start = ((), (), s32[]{:S(2)}) async-start(), calls=%async_computation.2 | async-start | bytes 17825792 | tf_op jit(solution)/shard_map/reduce_scatter | solution.py:46
Sparse Core Ops, SparseCore 0:
  273.9 97.7 reduce-scatter.1
where the time goes:
time: 384 us; the launch traced here: 381 us
  waiting for transfers between devices  288 us (75%)
  local copies, waits for them, and re-layouts  48 us (12%)
  between operations  13.5 us (4%)
  matrix products  12.8 us (3%)
  starting transfers between devices  10 us (3%)
  other arithmetic  8.72 us (2%)
    all_to_all x1, waiting for transfers between devices, body(): lax.all_to_all(jnp.take(blocks_local, picked, axis=1), 'feat', split_axis...  190 us
    reduce_scatter x1, waiting for transfers between devices, body(): lax.psum_scatter(jnp.einsum('tki,tkj->ikj', row_blocks, column_blocks, pr...  97.9 us
    mul x1, local copies, waits for them, and re-layouts, body(): jnp.einsum('tki,tkj->ikj', row_blocks, column_blocks, preferred_element_t...  18.5 us
    dot_general x1, matrix products, body(): jnp.einsum('tki,tkj->ikj', row_blocks, column_blocks, preferred_element_t...  12.8 us
    all_to_all x1, starting transfers between devices, body(): lax.all_to_all(jnp.take(blocks_local, picked, axis=1), 'feat', split_axis...  9.98 us
  transfers between devices with their start and end apart: 2, of which 2 were waited for; matrix products, arithmetic and copies ran while one was open for 1% of the time, Pallas kernels for 0%

commit v1 on v0

v1 whole, which is shorter than its diff:
```python
import jax
import jax.numpy as jnp
from jax import lax
from jax.sharding import PartitionSpec as P

BLK = 512
CHUNKS = 4


def body(activations, pattern, block_slot):
    tok_rows, width = activations.shape
    feat_count = lax.axis_size("feat")
    tok_count = lax.axis_size("tok")
    my_index = lax.axis_index("feat")
    panel_blocks = width // BLK
    list_length = pattern.shape[0]
    per_device = list_length // feat_count
    scale = 1.0 / (tok_rows * tok_count)
    ordered = jnp.zeros_like(pattern).at[block_slot].set(pattern)
    pairs = ordered.reshape(feat_count, per_device, 2)
    holder = pairs[:, :, 1] // panel_blocks
    local_column = pairs[:, :, 1] % panel_blocks
    match = holder == my_index
    picked = jnp.sum(jnp.where(match, local_column, 0), axis=1)
    my_pairs = lax.dynamic_index_in_dim(pairs, my_index, 0, keepdims=False)
    my_holder = my_pairs[:, 1] // panel_blocks
    blocks_local = activations.reshape(tok_rows, panel_blocks, BLK)
    row_blocks = jnp.take(blocks_local, my_pairs[:, 0] % panel_blocks, axis=1)
    w = BLK // CHUNKS
    outs = []
    for c in range(CHUNKS):
        part = blocks_local[:, :, c * w:(c + 1) * w]
        send = jnp.take(part, picked, axis=1)
        received = lax.all_to_all(send, "feat", split_axis=1, concat_axis=1, tiled=True)
        column_blocks = jnp.take(received, my_holder, axis=1)
        g = jnp.einsum("tki,tkj->ikj", row_blocks, column_blocks, preferred_element_type=jnp.float32) * scale
        outs.append(lax.psum_scatter(g, "tok", scatter_dimension=0, tiled=True))
    return jnp.concatenate(outs, axis=2)


def solution(mesh):
    placed = (P("tok", "feat"), P(), P())
    return jax.shard_map(
        body, mesh=mesh, in_specs=placed, out_specs=P("tok", "feat", None), check_vma=False
    )
```

time: 384 us -> 423 us (1.10)
  blocking collectives: 0 us -> 167 us
  waiting for transfers between devices: 288 us -> 137 us
  local copies, waits for them, and re-layouts: 48 us -> 61.9 us
  matrix products: 12.8 us -> 19 us
    all_to_all x0 -> x3, blocking collectives: none -> 167 us  [body(): lax.all_to_all(send, 'feat', split_axis=1, concat_axis=1, tiled=True)]
    all_to_all x1, waiting for transfers between devices: 190 us -> 43.3 us  [body(): lax.all_to_all(send, 'feat', split_axis=1, concat_axis=1, tiled=True)]
    gather x5 -> x8, local copies, waits for them, and re-layouts: 14 us -> 24.9 us  [the longest x4 14.4 us: body(): column_blocks = jnp.take(received, my_holder, axis=1)]
    dot_general x1 -> x4, matrix products: 12.8 us -> 19 us  [body(): jnp.einsum('tki,tkj->ikj', row_blocks, column_blocks, preferred_element_t...]
    unnamed x2 -> x8, local copies, waits for them, and re-layouts: 4.73 us -> 9.26 us
    mul x1 -> x4, local copies, waits for them, and re-layouts: 18.5 us -> 14 us  [body(): jnp.einsum('tki,tkj->ikj', row_blocks, column_blocks, preferred_element_t...]
    reduce_scatter x1 -> x4, waiting for transfers between devices: 97.9 us -> 94 us  [body(): outs.append(lax.psum_scatter(g, 'tok', scatter_dimension=0, tiled=True))]
  transfers between devices with their start and end apart: 2 -> 5, of which waited for: 2 -> 3; matrix products, arithmetic and copies ran while one was open for 1% -> 10% of each run, Pallas kernels for 0% -> 0%
where the time goes in v1:
time: 423 us; the launch traced here: 417 us
  blocking collectives  167 us (39%)
  waiting for transfers between devices  137 us (32%)
  local copies, waits for them, and re-layouts  61.9 us (15%)
  matrix products  19 us (4%)
  between operations  13.3 us (3%)
  starting transfers between devices  10.1 us (2%)
  other arithmetic  8.83 us (2%)
    all_to_all x3, blocking collectives, body(): lax.all_to_all(send, 'feat', split_axis=1, concat_axis=1, tiled=True)  167 us
    reduce_scatter x4, waiting for transfers between devices, body(): outs.append(lax.psum_scatter(g, 'tok', scatter_dimension=0, tiled=True))  94 us
    all_to_all x1, waiting for transfers between devices, body(): lax.all_to_all(send, 'feat', split_axis=1, concat_axis=1, tiled=True)  43.3 us
    dot_general x4, matrix products, body(): jnp.einsum('tki,tkj->ikj', row_blocks, column_blocks, preferred_element_t...  19 us
    gather x4, local copies, waits for them, and re-layouts, body(): column_blocks = jnp.take(received, my_holder, axis=1)  14.4 us
    mul x4, local copies, waits for them, and re-layouts, body(): jnp.einsum('tki,tkj->ikj', row_blocks, column_blocks, preferred_element_t...  14 us
    gather x4, local copies, waits for them, and re-layouts, body(): send = jnp.take(part, picked, axis=1)  10.6 us
    all_to_all x1, starting transfers between devices, body(): lax.all_to_all(send, 'feat', split_axis=1, concat_axis=1, tiled=True)  9.98 us
  transfers between devices with their start and end apart: 5, of which 3 were waited for; matrix products, arithmetic and copies ran while one was open for 10% of the time, Pallas kernels for 0%

profile of v1, /device:TPU:69, one launch (start us, length us, event | category | flops | bytes accessed | tf_op | source)
XLA Modules:
  0.0 417.4 jit_solution(13398491708162485194)
XLA Ops:
  9.4 3.9 copy.27
  17.6 3.2 gather_fusion.1
  20.8 3.2 gather_fusion.7
  28.2 7.0 %select_bitcast_fusion.3 = (bf16[512,16,128]{2,0,1:T(8,128)(2,1)}, bf16[512,16,128]{2,0,1:T(8,128)(2,1)}, bf16[512,16,128]{2,0,1:T(8,128)(2,1)}, bf16[512,16,128]{2,0,1:T(8,128)(2,1)}) fusion(bf16[16,512,128]{2,1,0:T(8,128)(2,1)} %gather_fusion.1, pred[16]{0:T(512)(128)(4,1)S(1)} %compare_and_fusion.1, bf16[16,512,128]{2,1,0:T(8,128)(2,1)} %gather_fusion.3, ...), kind=kLoop, calls=%fused_computation.26 | loop fusion | flops 4194304 | bytes 16777232 | tf_op jit(solution)/shard_map/jit(_take)/select_n | solution.py:33
  35.2 10.0 %all-to-all-start.3 = ((bf16[512,16,128]{2,0,1:T(8,128)(2,1)}), bf16[512,16,128]{2,0,1:T(8,128)(2,1)}, u32[]{:S(2)}, u32[]{:S(2)}) async-start(bf16[512,16,128]{2,0,1:T(8,128)(2,1)} %get-tuple-element.18), calls=%async_computation.6 | async-start | bytes 4194304 | tf_op jit(solution)/shard_map/all_to_all | solution.py:34
  45.3 4.2 gather_fusion
  49.5 43.3 %all-to-all-done.3 = bf16[512,16,128]{2,0,1:T(8,128)(2,1)} async-done(((bf16[512,16,128]{2,0,1:T(8,128)(2,1)}), bf16[512,16,128]{2,0,1:T(8,128)(2,1)}, u32[]{:S(2)}, u32[]{:S(2)}) %all-to-all-start.3) | async-done | bytes 2097184 | tf_op jit(solution)/shard_map/all_to_all | solution.py:34
  92.7 3.6 gather_fusion.8
  96.3 4.7 %multiply_bitcast_fusion = f32[512,12,128]{0,2,1:T(8,128)S(1)} fusion(bf16[12,512,128]{2,1,0:T(8,128)(2,1)} %gather_fusion.8, pred[12]{0:T(512)(128)(4,1)S(1)} %get-tuple-element.9, bf16[12,512,512]{2,1,0:T(8,128)(2,1)} %gather_fusion, pred[12]{0:T(512)(128)(4,1)S(1)} %get-tuple-element.6), kind=kOutput, calls=%fused_computation.19 | convolution fusion | flops 810024960 | bytes 11010072 | tf_op jit(solution)/shard_map/tki,tkj->ikj/dot_general | solution.py:36
  101.1 3.5 copy.40
  106.1 56.5 %all_to_all.20 = bf16[512,16,128]{2,0,1:T(8,128)(2,1)} all-to-all(bf16[512,16,128]{2,0,1:T(8,128)(2,1)S(1)} %copy-done.2), channel_id=1, replica_groups=mesh['feat'=16,'tok'=16] {'feat'}, dimensions={1} | all-to-all | bytes 4194304 | tf_op jit(solution)/shard_map/all_to_all | solution.py:34
  162.6 3.6 gather_fusion.6
  166.2 4.7 %multiply_bitcast_fusion.1 = f32[512,12,128]{0,2,1:T(8,128)S(1)} fusion(bf16[12,512,128]{2,1,0:T(8,128)(2,1)} %gather_fusion.6, pred[12]{0:T(512)(128)(4,1)S(1)} %get-tuple-element.9, bf16[12,512,512]{2,1,0:T(8,128)(2,1)} %gather_fusion, pred[12]{0:T(512)(128)(4,1)S(1)} %get-tuple-element.6), kind=kOutput, calls=%fused_computation.20 | convolution fusion | flops 810024960 | bytes 11010072 | tf_op jit(solution)/shard_map/tki,tkj->ikj/dot_general | solution.py:36
  171.0 3.5 copy.37
  176.0 55.0 %all_to_all.21 = bf16[512,16,128]{2,0,1:T(8,128)(2,1)} all-to-all(bf16[512,16,128]{2,0,1:T(8,128)(2,1)S(1)} %copy-done.1), channel_id=1, replica_groups=mesh['feat'=16,'tok'=16] {'feat'}, dimensions={1} | all-to-all | bytes 4194304 | tf_op jit(solution)/shard_map/all_to_all | solution.py:34
  231.0 3.6 gather_fusion.2
  234.6 4.8 %multiply_bitcast_fusion.3 = f32[512,12,128]{0,2,1:T(8,128)S(1)} fusion(bf16[12,512,128]{2,1,0:T(8,128)(2,1)} %gather_fusion.2, pred[12]{0:T(512)(128)(4,1)S(1)} %get-tuple-element.9, bf16[12,512,512]{2,1,0:T(8,128)(2,1)} %gather_fusion, pred[12]{0:T(512)(128)(4,1)S(1)} %get-tuple-element.6), kind=kOutput, calls=%fused_computation.22 | convolution fusion | flops 810024960 | bytes 11010072 | tf_op jit(solution)/shard_map/tki,tkj->ikj/dot_general | solution.py:36
  239.4 3.5 copy.31
  244.5 55.4 %all_to_all.22 = bf16[512,16,128]{2,0,1:T(8,128)(2,1)} all-to-all(bf16[512,16,128]{2,0,1:T(8,128)(2,1)S(1)} %copy-done), channel_id=1, replica_groups=mesh['feat'=16,'tok'=16] {'feat'}, dimensions={1} | all-to-all | bytes 4194304 | tf_op jit(solution)/shard_map/all_to_all | solution.py:34
  299.9 3.6 gather_fusion.4
  303.5 4.8 %multiply_bitcast_fusion.2 = f32[512,12,128]{0,2,1:T(8,128)S(1)} fusion(bf16[12,512,128]{2,1,0:T(8,128)(2,1)} %gather_fusion.4, pred[12]{0:T(512)(128)(4,1)S(1)} %get-tuple-element.9, bf16[12,512,512]{2,1,0:T(8,128)(2,1)} %gather_fusion, pred[12]{0:T(512)(128)(4,1)S(1)} %get-tuple-element.6), kind=kOutput, calls=%fused_computation.21 | convolution fusion | flops 810024960 | bytes 11010072 | tf_op jit(solution)/shard_map/tki,tkj->ikj/dot_general | solution.py:36
  308.3 3.5 copy.34
  313.9 23.8 %reduce-scatter.5.cloned.1.call-done = f32[32,12,128]{2,1,0:T(8,128)} async-done(((f32[512,12,128]{2,1,0:T(8,128)}), f32[32,12,128]{2,1,0:T(8,128)}) %reduce-scatter.5.cloned.1.call-update) | async-done | bytes 196624 | tf_op jit(solution)/shard_map/reduce_scatter | solution.py:37
  338.7 70.2 %reduce-scatter.7.cloned.1.call-done = f32[32,12,128]{2,1,0:T(8,128)} async-done(((f32[512,12,128]{2,1,0:T(8,128)}), f32[32,12,128]{2,1,0:T(8,128)}) %reduce-scatter.7.cloned.1.call-update) | async-done | bytes 196624 | tf_op jit(solution)/shard_map/reduce_scatter | solution.py:37
  (39 shorter events, 21.2 us)
Async XLA Ops:
  35.2 57.5 %all-to-all-start.3 = ((bf16[512,16,128]{2,0,1:T(8,128)(2,1)}), bf16[512,16,128]{2,0,1:T(8,128)(2,1)}, u32[]{:S(2)}, u32[]{:S(2)}) async-start(bf16[512,16,128]{2,0,1:T(8,128)(2,1)} %get-tuple-element.18), calls=%async_computation.6 | async-start | bytes 4194304 | tf_op jit(solution)/shard_map/all_to_all | solution.py:34
  45.2 266.7 %reduce-scatter.11.cloned.1.call-start = ((), (), s32[]{:S(2)}) async-start(), calls=%async_computation.11 | async-start | bytes 4456448 | tf_op jit(solution)/shard_map/reduce_scatter | solution.py:37
  104.5 1.6 copy-start.2
  104.6 208.3 %reduce-scatter.9.cloned.1.call-start = ((), (), s32[]{:S(2)}) async-start(), calls=%async_computation.10 | async-start | bytes 4456448 | tf_op jit(solution)/shard_map/reduce_scatter | solution.py:37
  174.4 1.6 copy-start.1
  174.5 163.3 %reduce-scatter.5.cloned.1.call-start = ((), (), s32[]{:S(2)}) async-start(), calls=%async_computation.8 | async-start | bytes 4456448 | tf_op jit(solution)/shard_map/reduce_scatter | solution.py:37
  242.9 1.6 copy-start
  243.0 166.0 %reduce-scatter.7.cloned.1.call-start = ((), (), s32[]{:S(2)}) async-start(), calls=%async_computation.9 | async-start | bytes 4456448 | tf_op jit(solution)/shard_map/reduce_scatter | solution.py:37
Sparse Core Ops, SparseCore 0:
  104.7 73.7 reduce-scatter.10
  181.0 78.6 reduce-scatter.8
  262.3 75.3 reduce-scatter.4
  340.1 68.7 reduce-scatter.6

commit v2 on v1

v2 whole, which is shorter than its diff:
```python
import functools

import jax
import jax.numpy as jnp
from jax import lax
from jax.experimental import pallas as pl
from jax.experimental.pallas import tpu as pltpu
from jax.sharding import PartitionSpec as P

BLK = 512
MESH = pl.DeviceIdType.MESH


def exchange_kernel(n, send_ref, recv_ref, send_sem, recv_sem, local_sem):
    me = lax.axis_index("feat")
    barrier = pltpu.get_barrier_semaphore()
    for k in range(1, n):
        peer = lax.rem(me + k, n)
        pl.semaphore_signal(barrier, 1, device_id={"feat": peer}, device_id_type=MESH)
    pl.semaphore_wait(barrier, n - 1)
    local = pltpu.make_async_copy(send_ref.at[me], recv_ref.at[me], local_sem)
    local.start()
    copies = []
    for k in range(1, n):
        peer = lax.rem(me + k, n)
        copy = pltpu.make_async_remote_copy(
            src_ref=send_ref.at[peer],
            dst_ref=recv_ref.at[me],
            send_sem=send_sem.at[k],
            recv_sem=recv_sem.at[k],
            device_id={"feat": peer},
            device_id_type=MESH,
        )
        copy.start()
        copies.append(copy)
    for copy in copies:
        copy.wait()
    local.wait()


def exchange(send):
    n = send.shape[0]
    return pl.pallas_call(
        functools.partial(exchange_kernel, n),
        out_shape=jax.ShapeDtypeStruct(send.shape, send.dtype),
        in_specs=[pl.BlockSpec(memory_space=pl.ANY)],
        out_specs=pl.BlockSpec(memory_space=pl.ANY),
        scratch_shapes=[
            pltpu.SemaphoreType.DMA((n,)),
            pltpu.SemaphoreType.DMA((n,)),
            pltpu.SemaphoreType.DMA,
        ],
        compiler_params=pltpu.CompilerParams(collective_id=0, has_side_effects=True),
    )(send)


def body(activations, pattern, block_slot):
    tok_rows, width = activations.shape
    feat_count = lax.axis_size("feat")
    tok_count = lax.axis_size("tok")
    my_index = lax.axis_index("feat")
    panel_blocks = width // BLK
    list_length = pattern.shape[0]
    per_device = list_length // feat_count
    scale = 1.0 / (tok_rows * tok_count)
    ordered = jnp.zeros_like(pattern).at[block_slot].set(pattern)
    pairs = ordered.reshape(feat_count, per_device, 2)
    holder = pairs[:, :, 1] // panel_blocks
    local_column = pairs[:, :, 1] % panel_blocks
    picked = jnp.sum(jnp.where(holder == my_index, local_column, 0), axis=1)
    my_pairs = lax.dynamic_index_in_dim(pairs, my_index, 0, keepdims=False)
    my_holder = my_pairs[:, 1] // panel_blocks
    blocks_local = activations.reshape(tok_rows, panel_blocks, BLK).transpose(1, 0, 2)
    row_blocks = jnp.take(blocks_local, my_pairs[:, 0] % panel_blocks, axis=0)
    send = jnp.take(blocks_local, picked, axis=0)
    received = exchange(send)
    column_blocks = jnp.take(received, my_holder, axis=0)
    g = jnp.einsum("kti,ktj->ikj", row_blocks, column_blocks, preferred_element_type=jnp.float32) * scale
    return lax.psum_scatter(g, "tok", scatter_dimension=0, tiled=True)


def solution(mesh):
    placed = (P("tok", "feat"), P(), P())
    return jax.shard_map(
        body, mesh=mesh, in_specs=placed, out_specs=P("tok", "feat", None), check_vma=False
    )
```

time: 423 us -> 388 us (0.917)
  Pallas kernels: 0 us -> 202 us
  blocking collectives: 167 us -> 0 us
  waiting for transfers between devices: 137 us -> 103 us
  local copies, waits for them, and re-layouts: 61.9 us -> 46.1 us
  starting transfers between devices: 10.1 us -> 0.01 us
  matrix products: 19 us -> 12.8 us
    pallas_call x0 -> x1, Pallas kernels: none -> 202 us  [exchange(): pl.pallas_call(functools.partial(exchange_kernel, n), out_shape=jax.Shape...]
    all_to_all x3 -> x0, blocking collectives: 167 us -> none  [body(): lax.all_to_all(send, 'feat', split_axis=1, concat_axis=1, tiled=True)]
    all_to_all x1 -> x0, waiting for transfers between devices: 43.3 us -> none  [body(): lax.all_to_all(send, 'feat', split_axis=1, concat_axis=1, tiled=True)]
    gather x9 -> x3, local copies, waits for them, and re-layouts: 29.1 us -> 16.3 us  [the longest x1 7.6 us: body(): column_blocks = jnp.take(received, my_holder, axis=0)]
    all_to_all x1 -> x0, starting transfers between devices: 9.98 us -> none  [body(): lax.all_to_all(send, 'feat', split_axis=1, concat_axis=1, tiled=True)]
    reduce_scatter x4 -> x1, waiting for transfers between devices: 94 us -> 103 us  [body(): return lax.psum_scatter(g, 'tok', scatter_dimension=0, tiled=True)]
    dot_general x4 -> x1, matrix products: 19 us -> 12.8 us  [body(): jnp.einsum('kti,ktj->ikj', row_blocks, column_blocks, preferred_element_t...]
    unnamed x8 -> x2, local copies, waits for them, and re-layouts: 9.26 us -> 4.73 us
  transfers between devices with their start and end apart: 5 -> 1, of which waited for: 3 -> 1; matrix products, arithmetic and copies ran while one was open for 10% -> 0% of each run, Pallas kernels for 0% -> 0%
where the time goes in v2:
time: 388 us; the launch traced here: 385 us
  Pallas kernels  202 us (52%)
  waiting for transfers between devices  103 us (27%)
  local copies, waits for them, and re-layouts  46.1 us (12%)
  between operations  13.5 us (3%)
  matrix products  12.8 us (3%)
  other arithmetic  8.32 us (2%)
    pallas_call x1, Pallas kernels, exchange(): pl.pallas_call(functools.partial(exchange_kernel, n), out_shape=jax.Shape...  202 us
    reduce_scatter x1, waiting for transfers between devices, body(): return lax.psum_scatter(g, 'tok', scatter_dimension=0, tiled=True)  103 us
    mul x1, local copies, waits for them, and re-layouts, body(): jnp.einsum('kti,ktj->ikj', row_blocks, column_blocks, preferred_element_t...  18.5 us
    dot_general x1, matrix products, body(): jnp.einsum('kti,ktj->ikj', row_blocks, column_blocks, preferred_element_t...  12.8 us
  transfers between devices with their start and end apart: 1, of which 1 were waited for; matrix products, arithmetic and copies ran while one was open for 0% of the time, Pallas kernels for 0%

profile of v2, /device:TPU:69, one launch (start us, length us, event | category | flops | bytes accessed | tf_op | source)
XLA Modules:
  0.0 385.3 jit_solution(13451650276684516298)
XLA Ops:
  6.5 0.0 reduce-scatter.2.cloned.1.call-start
  6.5 0.7 compare_select_fusion
  7.2 0.8 copy.16
  8.0 1.0 scatter_custom_fusion
  9.1 0.1 copy.17
  9.1 0.1 reshape.32
  9.2 0.1 fusion.14
  9.5 3.9 %copy.18 = bf16[512,2048]{0,1:T(8,128)(2,1)} copy(bf16[512,2048]{1,0:T(8,128)(2,1)} %param.3) | data formatting | bytes 4194304 | tf_op args[0]
  13.4 2.8 copy.19
  16.2 4.1 %gather_fusion.2 = bf16[12,512,512]{2,1,0:T(8,128)(2,1)} fusion(bf16[4,512,512]{2,1,0:T(8,128)(2,1)S(1)} %bitcast.22, s32[1024]{0:T(1024)S(1)} %pad_clamp_fusion), kind=kCustom, calls=%fused_computation.2 | custom fusion | bytes 12582960 | tf_op jit(solution)/shard_map/jit(_take)/gather | solution.py:74
  20.3 4.6 %gather_fusion = bf16[16,512,512]{2,1,0:T(8,128)(2,1)} fusion(bf16[4,512,512]{2,1,0:T(8,128)(2,1)S(1)} %bitcast.23, s32[1024]{0:T(1024)S(1)} %pad_clamp_fusion.2), kind=kCustom, calls=%fused_computation | custom fusion | bytes 16777280 | tf_op jit(solution)/shard_map/jit(_take)/gather | solution.py:75
  24.9 7.5 %broadcast_select_fusion.send_ref = bf16[16,512,512]{2,1,0:T(8,128)(2,1)} fusion(bf16[16,512,512]{2,1,0:T(8,128)(2,1)} %gather_fusion, pred[16]{0:T(512)(128)(4,1)S(1)} %compare_and_fusion), kind=kLoop, calls=%fused_computation.5 | loop fusion | flops 4194304 | bytes 16777232 | tf_op jit(solution)/shard_map/jit(_take)/select_n | solution.py:75
  32.4 201.8 %shard_map.37 = bf16[16,512,512]{2,1,0:T(8,128)(2,1)} custom-call(bf16[16,512,512]{2,1,0:T(8,128)(2,1)} %broadcast_select_fusion.send_ref), custom_call_target="tpu_custom_call" | custom-call | tf_op jit(solution)/shard_map/pallas_call | solution.py:43
  234.2 7.6 %gather_fusion.1 = bf16[12,512,512]{2,1,0:T(8,128)(2,1)} fusion(bf16[16,512,512]{2,1,0:T(8,128)(2,1)} %shard_map.37, s32[1024]{0:T(1024)S(1)} %pad_clamp_fusion.1), kind=kCustom, calls=%fused_computation.1 | custom fusion | bytes 12582960 | tf_op jit(solution)/shard_map/jit(_take)/gather | solution.py:77
  241.8 12.8 %multiply_bitcast_fusion = f32[512,12,512]{0,2,1:T(8,128)} fusion(bf16[12,512,512]{2,1,0:T(8,128)(2,1)} %gather_fusion.2, pred[12]{0:T(512)(128)(4,1)S(1)} %get-tuple-element.9, bf16[12,512,512]{2,1,0:T(8,128)(2,1)} %gather_fusion.1, pred[12]{0:T(512)(128)(4,1)S(1)} %get-tuple-element.5), kind=kOutput, calls=%fused_computation.4 | convolution fusion | flops 3230662656 | bytes 25165848 | tf_op jit(solution)/shard_map/kti,ktj->ikj/dot_general | solution.py:78
  254.6 18.5 %copy.21 = f32[512,12,512]{2,1,0:T(8,128)} copy(f32[512,12,512]{0,2,1:T(8,128)} %multiply_bitcast_fusion) | data formatting | bytes 25165824 | tf_op jit(solution)/shard_map/mul | solution.py:78
  273.1 0.0 reduce-scatter.2.cloned.1.call-update
  273.1 102.8 %reduce-scatter.2.cloned.1.call-done = f32[32,12,512]{2,1,0:T(8,128)} async-done(((f32[512,12,512]{2,1,0:T(8,128)}), f32[32,12,512]{2,1,0:T(8,128)}) %reduce-scatter.2.cloned.1.call-update) | async-done | bytes 786448 | tf_op jit(solution)/shard_map/reduce_scatter | solution.py:79
  375.9 2.6 copy.22
  (7 shorter events, 0.1 us)
Async XLA Ops:
  6.5 369.3 %reduce-scatter.2.cloned.1.call-start = ((), (), s32[]{:S(2)}) async-start(), calls=%async_computation.1 | async-start | bytes 17825792 | tf_op jit(solution)/shard_map/reduce_scatter | solution.py:79
Sparse Core Ops, SparseCore 0:
  273.2 102.6 reduce-scatter.1

commit v3 on v1

v3 whole, which is shorter than its diff:
```python
import functools

import jax
import jax.numpy as jnp
from jax import lax
from jax.experimental import pallas as pl
from jax.experimental.pallas import tpu as pltpu
from jax.sharding import PartitionSpec as P

BLK = 512
CHUNKS = 4
MESH = pl.DeviceIdType.MESH


def fused_kernel(n_feat, n_tok, chunks, scale,
                 holder_ref, send_ref, rows_ref, out_ref, *scratch):
    recv = scratch[:chunks]
    gbuf, sta, stb, accbuf, fsend, frecv, flocal, asend, arecv, alocal, bsend, brecv = scratch[chunks:]
    slots, width, tokens = rows_ref.shape
    w = width // chunks
    group = n_tok // 2
    piece = width // n_tok
    me = lax.axis_index("feat")
    t = lax.axis_index("tok")
    x = t // group
    j = t % group
    partner = (1 - x) * group + j

    barrier = pltpu.get_barrier_semaphore()
    for k in range(1, n_feat):
        pl.semaphore_signal(barrier, 1, device_id={"feat": lax.rem(me + k, n_feat)}, device_id_type=MESH)
    for o in range(1, group):
        pl.semaphore_signal(barrier, 1, device_id={"tok": x * group + lax.rem(j + o, group)}, device_id_type=MESH)
    pl.semaphore_signal(barrier, 1, device_id={"tok": partner}, device_id_type=MESH)
    pl.semaphore_wait(barrier, n_feat - 1 + group - 1 + 1)

    def feat_copies(c):
        cols = pl.ds(c * w, w)
        local = pltpu.make_async_copy(send_ref.at[me, :, cols], recv[c].at[me], flocal.at[c])
        copies = [local]
        for k in range(1, n_feat):
            peer = lax.rem(me + k, n_feat)
            copies.append(pltpu.make_async_remote_copy(
                src_ref=send_ref.at[peer, :, cols],
                dst_ref=recv[c].at[me],
                send_sem=fsend.at[c, k],
                recv_sem=frecv.at[c, k],
                device_id={"feat": peer},
                device_id_type=MESH,
            ))
        return copies

    pending = feat_copies(0)
    for cp in pending:
        cp.start()
    for c in range(chunks):
        for cp in pending:
            cp.wait()
        if c + 1 < chunks:
            pending = feat_copies(c + 1)
            for cp in pending:
                cp.start()

        def gram_one(k, carry):
            q = recv[c][holder_ref[k]]
            g = jnp.dot(rows_ref[k], q, preferred_element_type=jnp.float32) * scale
            for xx in range(2):
                for m in range(group):
                    r0 = (xx * group + m) * piece
                    gbuf[m, xx, k] = g[r0:r0 + piece, :]
            return carry

        lax.fori_loop(0, slots, gram_one, 0)

        own = pltpu.make_async_copy(gbuf.at[j], sta.at[c, j], alocal.at[c])
        own.start()
        a_copies = []
        for o in range(1, group):
            dest = lax.rem(j + o, group)
            cp = pltpu.make_async_remote_copy(
                src_ref=gbuf.at[dest],
                dst_ref=sta.at[c, j],
                send_sem=asend.at[c, o],
                recv_sem=arecv.at[c, o],
                device_id={"tok": x * group + dest},
                device_id_type=MESH,
            )
            cp.start()
            a_copies.append(cp)
        own.wait()
        for cp in a_copies:
            cp.wait()
        acc = sta[c, 0]
        for m in range(1, group):
            acc = acc + sta[c, m]
        accbuf[...] = acc
        bcp = pltpu.make_async_remote_copy(
            src_ref=accbuf.at[1 - x],
            dst_ref=stb.at[c],
            send_sem=bsend.at[c],
            recv_sem=brecv.at[c],
            device_id={"tok": partner},
            device_id_type=MESH,
        )
        bcp.start()
        bcp.wait()
        out_ref[:, :, pl.ds(c * w, w)] = accbuf[x] + stb[c]


def fused(holder, send, rows_t, n_feat, n_tok, scale):
    slots, width, tokens = rows_t.shape
    w = width // CHUNKS
    group = n_tok // 2
    piece = width // n_tok
    kernel = functools.partial(fused_kernel, n_feat, n_tok, CHUNKS, scale)
    return pl.pallas_call(
        kernel,
        out_shape=jax.ShapeDtypeStruct((slots, piece, width), jnp.float32),
        in_specs=[
            pl.BlockSpec(memory_space=pltpu.SMEM),
            pl.BlockSpec(memory_space=pl.ANY),
            pl.BlockSpec(memory_space=pltpu.VMEM),
        ],
        out_specs=pl.BlockSpec(memory_space=pltpu.VMEM),
        scratch_shapes=[pltpu.VMEM((n_feat, tokens, w), send.dtype) for _ in range(CHUNKS)] + [
            pltpu.VMEM((group, 2, slots, piece, w), jnp.float32),
            pltpu.VMEM((CHUNKS, group, 2, slots, piece, w), jnp.float32),
            pltpu.VMEM((CHUNKS, slots, piece, w), jnp.float32),
            pltpu.VMEM((2, slots, piece, w), jnp.float32),
            pltpu.SemaphoreType.DMA((CHUNKS, n_feat)),
            pltpu.SemaphoreType.DMA((CHUNKS, n_feat)),
            pltpu.SemaphoreType.DMA((CHUNKS,)),
            pltpu.SemaphoreType.DMA((CHUNKS, group)),
            pltpu.SemaphoreType.DMA((CHUNKS, group)),
            pltpu.SemaphoreType.DMA((CHUNKS,)),
            pltpu.SemaphoreType.DMA((CHUNKS,)),
            pltpu.SemaphoreType.DMA((CHUNKS,)),
        ],
        compiler_params=pltpu.CompilerParams(
            collective_id=0, has_side_effects=True, vmem_limit_bytes=60 * 1024 * 1024
        ),
    )(holder, send, rows_t)


def body(activations, pattern, block_slot):
    tok_rows, width = activations.shape
    feat_count = lax.axis_size("feat")
    tok_count = lax.axis_size("tok")
    my_index = lax.axis_index("feat")
    panel_blocks = width // BLK
    list_length = pattern.shape[0]
    per_device = list_length // feat_count
    scale = 1.0 / (tok_rows * tok_count)
    ordered = jnp.zeros_like(pattern).at[block_slot].set(pattern)
    pairs = ordered.reshape(feat_count, per_device, 2)
    holder = pairs[:, :, 1] // panel_blocks
    local_column = pairs[:, :, 1] % panel_blocks
    picked = jnp.sum(jnp.where(holder == my_index, local_column, 0), axis=1)
    my_pairs = lax.dynamic_index_in_dim(pairs, my_index, 0, keepdims=False)
    my_holder = my_pairs[:, 1] // panel_blocks
    blocks_local = activations.reshape(tok_rows, panel_blocks, BLK).transpose(1, 0, 2)
    rows_t = jnp.take(blocks_local, my_pairs[:, 0] % panel_blocks, axis=0).transpose(0, 2, 1)
    send = jnp.take(blocks_local, picked, axis=0)
    out = fused(my_holder, send, rows_t, feat_count, tok_count, scale)
    return out.transpose(1, 0, 2)


def solution(mesh):
    placed = (P("tok", "feat"), P(), P())
    return jax.shard_map(
        body, mesh=mesh, in_specs=placed, out_specs=P("tok", "feat", None), check_vma=False
    )
```

time: 423 us -> 303 us (0.72)
  Pallas kernels: 0 us -> 256 us
  blocking collectives: 167 us -> 0 us
  waiting for transfers between devices: 137 us -> 0 us
  local copies, waits for them, and re-layouts: 61.9 us -> 28.3 us
  matrix products: 19 us -> 0 us
  between operations: 13.3 us -> 0.09 us
  starting transfers between devices: 10.1 us -> 0 us
  other arithmetic: 8.83 us -> 15 us
    pallas_call x0 -> x1, Pallas kernels: none -> 256 us  [fused(): pl.pallas_call(kernel, out_shape=jax.ShapeDtypeStruct((slots, piece, widt...]
    all_to_all x3 -> x0, blocking collectives: 167 us -> none  [body(): lax.all_to_all(send, 'feat', split_axis=1, concat_axis=1, tiled=True)]
    reduce_scatter x4 -> x0, waiting for transfers between devices: 94 us -> none  [body(): outs.append(lax.psum_scatter(g, 'tok', scatter_dimension=0, tiled=True))]
    all_to_all x1 -> x0, waiting for transfers between devices: 43.3 us -> none  [body(): lax.all_to_all(send, 'feat', split_axis=1, concat_axis=1, tiled=True)]
    dot_general x4 -> x0, matrix products: 19 us -> none  [body(): jnp.einsum('tki,tkj->ikj', row_blocks, column_blocks, preferred_element_t...]
    mul x4 -> x0, local copies, waits for them, and re-layouts: 14 us -> none  [body(): jnp.einsum('tki,tkj->ikj', row_blocks, column_blocks, preferred_element_t...]
    gather x9 -> x3, local copies, waits for them, and re-layouts: 29.1 us -> 17.5 us  [the longest x2 12.8 us: body(): jnp.take(blocks_local, my_pairs[:, 0] % panel_blocks, axis=0)]
    all_to_all x1 -> x0, starting transfers between devices: 9.98 us -> none  [body(): lax.all_to_all(send, 'feat', split_axis=1, concat_axis=1, tiled=True)]
  transfers between devices with their start and end apart: 5 -> 0, of which waited for: 3 -> 0; matrix products, arithmetic and copies ran while one was open for 10% -> 0% of each run, Pallas kernels for 0% -> 0%
where the time goes in v3:
time: 303 us; the launch traced here: 300 us
  Pallas kernels  256 us (84%)
  local copies, waits for them, and re-layouts  28.3 us (9%)
  other arithmetic  15 us (5%)
    pallas_call x1, Pallas kernels, fused(): pl.pallas_call(kernel, out_shape=jax.ShapeDtypeStruct((slots, piece, widt...  256 us
    gather x2, local copies, waits for them, and re-layouts, body(): jnp.take(blocks_local, my_pairs[:, 0] % panel_blocks, axis=0)  12.8 us
    select_n x2, other arithmetic, body(): send = jnp.take(blocks_local, picked, axis=0)  7.47 us
    unnamed x3, local copies, waits for them, and re-layouts  6.8 us
    select_n x1, other arithmetic, body(): jnp.take(blocks_local, my_pairs[:, 0] % panel_blocks, axis=0)  6.16 us

profile of v3, /device:TPU:69, one launch (start us, length us, event | category | flops | bytes accessed | tf_op | source)
XLA Modules:
  0.0 299.7 jit_solution(16635209453698133205)
XLA Ops:
  0.0 0.7 compare_select_fusion
  0.7 0.8 copy.7
  1.5 1.0 scatter_custom_fusion
  2.5 0.1 copy.8
  2.6 0.1 reshape.28
  2.7 0.1 fusion.4
  2.9 0.5 and_select_fusion.1.holder_ref
  3.4 3.9 %copy.9 = bf16[512,2048]{0,1:T(8,128)(2,1)} copy(bf16[512,2048]{1,0:T(8,128)(2,1)} %param.3) | data formatting | bytes 4194304 | tf_op args[0]
  7.4 2.8 copy.10
  10.2 4.1 %gather_fusion.1 = bf16[12,512,512]{2,1,0:T(8,128)(2,1)} fusion(bf16[4,512,512]{2,1,0:T(8,128)(2,1)S(1)} %bitcast.28, s32[1024]{0:T(1024)S(1)} %pad_clamp_fusion), kind=kCustom, calls=%fused_computation.1 | custom fusion | bytes 12582960 | tf_op jit(solution)/shard_map/jit(_take)/gather | solution.py:162
  14.3 8.6 %copy.11 = bf16[12,512,512]{1,2,0:T(8,128)(2,1)} copy(bf16[12,512,512]{2,1,0:T(8,128)(2,1)} %gather_fusion.1) | data formatting | bytes 12582912 | tf_op jit(solution)/shard_map/jit(_take)/gather | solution.py:162
  22.9 6.2 %select_bitcast_fusion.rows_ref = bf16[12,512,512]{2,1,0:T(8,128)(2,1)} fusion(bf16[12,512,512]{1,2,0:T(8,128)(2,1)} %copy.11, pred[12]{0:T(512)(128)(4,1)S(1)} %get-tuple-element.5), kind=kLoop, calls=%fused_computation.4 | loop fusion | flops 3145728 | bytes 12582924 | tf_op jit(solution)/shard_map/jit(_take)/select_n | solution.py:162
  29.1 4.7 %gather_fusion = bf16[16,512,512]{2,1,0:T(8,128)(2,1)} fusion(bf16[4,512,512]{2,1,0:T(8,128)(2,1)S(1)} %bitcast.29, s32[1024]{0:T(1024)S(1)} %pad_clamp_fusion.1), kind=kCustom, calls=%fused_computation | custom fusion | bytes 16777280 | tf_op jit(solution)/shard_map/jit(_take)/gather | solution.py:163
  33.8 7.5 %broadcast_select_fusion.send_ref = bf16[16,512,512]{2,1,0:T(8,128)(2,1)} fusion(bf16[16,512,512]{2,1,0:T(8,128)(2,1)} %gather_fusion, pred[16]{0:T(512)(128)(4,1)S(1)} %compare_and_fusion), kind=kLoop, calls=%fused_computation.3 | loop fusion | flops 4194304 | bytes 16777232 | tf_op jit(solution)/shard_map/jit(_take)/select_n | solution.py:163
  41.3 256.3 %shard_map.37 = f32[12,32,512]{2,1,0:T(8,128)} custom-call(s32[12]{0:T(128)} %and_select_fusion.1.holder_ref, bf16[16,512,512]{2,1,0:T(8,128)(2,1)} %broadcast_select_fusion.send_ref, bf16[12,512,512]{2,1,0:T(8,128)(2,1)} %select_bitcast_fusion.rows_ref), custom_call_target="tpu_custom_call" | custom-call | tf_op jit(solution)/shard_map/pallas_call | solution.py:116
  297.6 2.1 copy.13
  (6 shorter events, 0.0 us)

commit v4 on v3

--- a/solution.py
+++ b/solution.py
@@ -13,10 +13,11 @@
 
 
 def fused_kernel(n_feat, n_tok, chunks, scale,
-                 holder_ref, send_ref, rows_ref, out_ref, *scratch):
+                 holder_ref, rowblk_ref, send_ref, act_ref, out_ref, *scratch):
     recv = scratch[:chunks]
     gbuf, sta, stb, accbuf, fsend, frecv, flocal, asend, arecv, alocal, bsend, brecv = scratch[chunks:]
-    slots, width, tokens = rows_ref.shape
+    slots = holder_ref.shape[0]
+    tokens, width = send_ref.shape[1], send_ref.shape[2]
     w = width // chunks
     group = n_tok // 2
     piece = width // n_tok
@@ -63,7 +64,10 @@
 
         def gram_one(k, carry):
             q = recv[c][holder_ref[k]]
-            g = jnp.dot(rows_ref[k], q, preferred_element_type=jnp.float32) * scale
+            p = act_ref[rowblk_ref[k]]
+            g = lax.dot_general(
+                p, q, (((0,), (0,)), ((), ())), preferred_element_type=jnp.float32
+            ) * scale
             for xx in range(2):
                 for m in range(group):
                     r0 = (xx * group + m) * piece
@@ -107,8 +111,9 @@
         out_ref[:, :, pl.ds(c * w, w)] = accbuf[x] + stb[c]
 
 
-def fused(holder, send, rows_t, n_feat, n_tok, scale):
-    slots, width, tokens = rows_t.shape
+def fused(holder, rowblk, send, activations, n_feat, n_tok, scale):
+    slots = holder.shape[0]
+    tokens, width = send.shape[1], send.shape[2]
     w = width // CHUNKS
     group = n_tok // 2
     piece = width // n_tok
@@ -117,6 +122,7 @@
         kernel,
         out_shape=jax.ShapeDtypeStruct((slots, piece, width), jnp.float32),
         in_specs=[
+            pl.BlockSpec(memory_space=pltpu.SMEM),
             pl.BlockSpec(memory_space=pltpu.SMEM),
             pl.BlockSpec(memory_space=pl.ANY),
             pl.BlockSpec(memory_space=pltpu.VMEM),
@@ -139,7 +145,7 @@
         compiler_params=pltpu.CompilerParams(
             collective_id=0, has_side_effects=True, vmem_limit_bytes=60 * 1024 * 1024
         ),
-    )(holder, send, rows_t)
+    )(holder, rowblk, send, activations)
 
 
 def body(activations, pattern, block_slot):
@@ -158,10 +164,12 @@
     picked = jnp.sum(jnp.where(holder == my_index, local_column, 0), axis=1)
     my_pairs = lax.dynamic_index_in_dim(pairs, my_index, 0, keepdims=False)
     my_holder = my_pairs[:, 1] // panel_blocks
+    send = jnp.stack(
+        [lax.dynamic_slice_in_dim(activations, picked[p] * BLK, BLK, axis=1) for p in range(feat_count)]
+    )
+    rowblk = my_pairs[:, 0] % panel_blocks
     blocks_local = activations.reshape(tok_rows, panel_blocks, BLK).transpose(1, 0, 2)
-    rows_t = jnp.take(blocks_local, my_pairs[:, 0] % panel_blocks, axis=0).transpose(0, 2, 1)
-    send = jnp.take(blocks_local, picked, axis=0)
-    out = fused(my_holder, send, rows_t, feat_count, tok_count, scale)
+    out = fused(my_holder, rowblk, send, blocks_local, feat_count, tok_count, scale)
     return out.transpose(1, 0, 2)
 
 

time: 303 us -> 314 us (1.036)
  other arithmetic: 15 us -> 1.35 us
  local copies, waits for them, and re-layouts: 28.3 us -> 41.8 us
  between operations: 0.09 us -> 10.1 us
    unnamed x3 -> x20, local copies, waits for them, and re-layouts: 6.8 us -> 33.8 us
    gather x3 -> x0, local copies, waits for them, and re-layouts: 17.5 us -> none  [the longest x2 12.8 us: body(): jnp.take(blocks_local, my_pairs[:, 0] % panel_blocks, axis=0)]
    select_n x4 -> x1, other arithmetic: 14.2 us -> 0.55 us  [body(): rowblk = my_pairs[:, 0] % panel_blocks]
where the time goes in v4:
time: 314 us; the launch traced here: 311 us
  Pallas kernels  257 us (82%)
  local copies, waits for them, and re-layouts  41.8 us (13%)
  between operations  10.1 us (3%)
    pallas_call x1, Pallas kernels, fused(): pl.pallas_call(kernel, out_shape=jax.ShapeDtypeStruct((slots, piece, widt...  257 us
    unnamed x20, local copies, waits for them, and re-layouts  33.8 us

profile of v4, /device:TPU:69, one launch (start us, length us, event | category | flops | bytes accessed | tf_op | source)
XLA Modules:
  0.0 310.8 jit_solution(5334967425943082638)
XLA Ops:
  0.0 0.7 compare_select_fusion
  0.7 0.8 copy.4
  1.5 1.0 scatter_custom_fusion
  3.4 0.7 fusion.8
  4.7 2.0 bitcast_dynamic-update-slice_fusion.15
  7.3 1.9 bitcast_dynamic-update-slice_fusion.14
  9.9 1.9 bitcast_dynamic-update-slice_fusion.13
  12.4 1.9 bitcast_dynamic-update-slice_fusion.12
  14.9 1.9 bitcast_dynamic-update-slice_fusion.11
  17.5 1.9 bitcast_dynamic-update-slice_fusion.10
  20.0 1.9 bitcast_dynamic-update-slice_fusion.9
  22.6 1.9 bitcast_dynamic-update-slice_fusion.8
  25.1 1.9 bitcast_dynamic-update-slice_fusion.7
  27.6 1.9 bitcast_dynamic-update-slice_fusion.6
  30.2 1.9 bitcast_dynamic-update-slice_fusion.5
  32.6 1.9 bitcast_dynamic-update-slice_fusion.4
  35.2 1.9 bitcast_dynamic-update-slice_fusion.3
  37.6 1.9 bitcast_dynamic-update-slice_fusion.2
  40.2 1.9 bitcast_dynamic-update-slice_fusion.1
  42.6 1.9 bitcast_dynamic-update-slice_fusion.send_ref
  44.5 2.5 copy.6
  47.0 4.2 %copy.7 = bf16[512,4,512]{2,0,1:T(8,128)(2,1)} copy(bf16[512,4,512]{0,2,1:T(8,128)(2,1)} %bitcast.68) | data formatting | bytes 4194304 | tf_op jit(solution)/shard_map/reshape | solution.py:171
  51.2 257.5 %shard_map.37 = f32[12,32,512]{2,1,0:T(8,128)} custom-call(s32[12]{0:T(128)} %get-tuple-element.6.holder_ref, s32[12]{0:T(128)} %get-tuple-element.5.rowblk_ref, bf16[16,512,512]{2,1,0:T(8,128)(2,1)} %bitcast_dynamic-update-slice_fusion.send_ref, bf16[4,512,512]{2,1,0:T(8,128)(2,1)} %bitcast.69), custom_call_target="tpu_custom_call" | custom-call | tf_op jit(solution)/shard_map/pallas_call | solution.py:121
  308.7 2.1 copy.24
  (7 shorter events, 0.8 us)
Async XLA Ops:
  4.7 39.8 %copy-start = (bf16[512,2048]{1,0:T(8,128)(2,1)S(1)}, bf16[512,2048]{1,0:T(8,128)(2,1)}, u32[]{:S(2)}) copy-start(bf16[512,2048]{1,0:T(8,128)(2,1)} %param.3) | copy-start | bytes 6291460

commit v5 on v4

--- a/solution.py
+++ b/solution.py
@@ -148,6 +148,25 @@
     )(holder, rowblk, send, activations)
 
 
+def gather_kernel(index_ref, src_ref, dst_ref):
+    dst_ref[0] = src_ref[...]
+
+
+def gather_blocks(activations, index):
+    tokens = activations.shape[0]
+    count = index.shape[0]
+    return pl.pallas_call(
+        gather_kernel,
+        out_shape=jax.ShapeDtypeStruct((count, tokens, BLK), activations.dtype),
+        grid_spec=pltpu.PrefetchScalarGridSpec(
+            num_scalar_prefetch=1,
+            grid=(count,),
+            in_specs=[pl.BlockSpec((tokens, BLK), lambda p, index_ref: (0, index_ref[p]))],
+            out_specs=pl.BlockSpec((1, tokens, BLK), lambda p, index_ref: (p, 0, 0)),
+        ),
+    )(index, activations)
+
+
 def body(activations, pattern, block_slot):
     tok_rows, width = activations.shape
     feat_count = lax.axis_size("feat")
@@ -164,11 +183,9 @@
     picked = jnp.sum(jnp.where(holder == my_index, local_column, 0), axis=1)
     my_pairs = lax.dynamic_index_in_dim(pairs, my_index, 0, keepdims=False)
     my_holder = my_pairs[:, 1] // panel_blocks
-    send = jnp.stack(
-        [lax.dynamic_slice_in_dim(activations, picked[p] * BLK, BLK, axis=1) for p in range(feat_count)]
-    )
+    send = gather_blocks(activations, picked)
     rowblk = my_pairs[:, 0] % panel_blocks
-    blocks_local = activations.reshape(tok_rows, panel_blocks, BLK).transpose(1, 0, 2)
+    blocks_local = gather_blocks(activations, jnp.arange(panel_blocks, dtype=jnp.int32))
     out = fused(my_holder, rowblk, send, blocks_local, feat_count, tok_count, scale)
     return out.transpose(1, 0, 2)
 

time: 314 us -> 283 us (0.901)
  local copies, waits for them, and re-layouts: 41.8 us -> 4.55 us
  Pallas kernels: 257 us -> 276 us
  between operations: 10.1 us -> 0.04 us
    unnamed x20 -> x2, local copies, waits for them, and re-layouts: 33.8 us -> 2.85 us
    pallas_call x0 -> x2, Pallas kernels: none -> 15.3 us  [gather_blocks(): pl.pallas_call(gather_kernel, out_shape=jax.ShapeDtypeStruct((count, toke...]
    reshape x1 -> x0, local copies, waits for them, and re-layouts: 4.18 us -> none  [body(): activations.reshape(tok_rows, panel_blocks, BLK).transpose(1, 0, 2)]
    pallas_call x1, Pallas kernels: 257 us -> 261 us  [fused(): pl.pallas_call(kernel, out_shape=jax.ShapeDtypeStruct((slots, piece, widt...]
where the time goes in v5:
time: 283 us
  Pallas kernels  276 us (98%)
  local copies, waits for them, and re-layouts  4.55 us (2%)
    pallas_call x1, Pallas kernels, fused(): pl.pallas_call(kernel, out_shape=jax.ShapeDtypeStruct((slots, piece, widt...  261 us
    pallas_call x2, Pallas kernels, gather_blocks(): pl.pallas_call(gather_kernel, out_shape=jax.ShapeDtypeStruct((count, toke...  15.3 us

profile of v5, /device:TPU:69, one launch (start us, length us, event | category | flops | bytes accessed | tf_op | source)
XLA Modules:
  0.0 282.7 jit_solution(3337693844959441443)
XLA Ops:
  0.0 0.5 iota.3.index_ref
  0.5 0.7 compare_select_fusion
  1.2 0.8 copy.4
  2.0 1.0 scatter_custom_fusion
  3.0 0.1 copy.5
  3.1 0.1 reshape.3
  3.2 0.7 fusion.4.index_ref
  3.9 0.6 and_select_fusion
  4.5 4.5 %shard_map.38.act_ref = bf16[4,512,512]{2,1,0:T(8,128)(2,1)} custom-call(s32[4]{0:T(128)} %iota.3.index_ref, bf16[512,2048]{1,0:T(8,128)(2,1)} %src_ref.3), custom_call_target="tpu_custom_call" | custom-call | tf_op jit(solution)/shard_map/pallas_call | solution.py:158
  9.0 10.8 %shard_map.37.send_ref = bf16[16,512,512]{2,1,0:T(8,128)(2,1)} custom-call(s32[16]{0:T(128)} %fusion.4.index_ref, bf16[512,2048]{1,0:T(8,128)(2,1)} %src_ref.3), custom_call_target="tpu_custom_call" | custom-call | tf_op jit(solution)/shard_map/pallas_call | solution.py:158
  19.7 260.9 %shard_map.39 = f32[12,32,512]{2,1,0:T(8,128)} custom-call(s32[12]{0:T(128)} %get-tuple-element.6.holder_ref, s32[12]{0:T(128)} %get-tuple-element.5.rowblk_ref, bf16[16,512,512]{2,1,0:T(8,128)(2,1)} %shard_map.37.send_ref, bf16[4,512,512]{2,1,0:T(8,128)(2,1)} %shard_map.38.act_ref), custom_call_target="tpu_custom_call" | custom-call | tf_op jit(solution)/shard_map/pallas_call | solution.py:121
  280.6 2.1 copy.7
  (1 shorter events, 0.0 us)

commit v6 on v5

--- a/solution.py
+++ b/solution.py
@@ -15,25 +15,30 @@
 def fused_kernel(n_feat, n_tok, chunks, scale,
                  holder_ref, rowblk_ref, send_ref, act_ref, out_ref, *scratch):
     recv = scratch[:chunks]
-    gbuf, sta, stb, accbuf, fsend, frecv, flocal, asend, arecv, alocal, bsend, brecv = scratch[chunks:]
+    (gbuf, st0, s1buf, st1, s2buf, st2,
+     fsend, frecv, flocal, send0, recv0, send1, recv1, send2, recv2) = scratch[chunks:]
     slots = holder_ref.shape[0]
     tokens, width = send_ref.shape[1], send_ref.shape[2]
     w = width // chunks
-    group = n_tok // 2
+    n_y = n_tok // 4
     piece = width // n_tok
     me = lax.axis_index("feat")
     t = lax.axis_index("tok")
-    x = t // group
-    j = t % group
-    partner = (1 - x) * group + j
+    x = t // (2 * n_y)
+    y = (t // 2) % n_y
+    core = t % 2
+    core_peer = t + 1 - 2 * core
+    x_peer = t + (1 - 2 * x) * 2 * n_y
 
     barrier = pltpu.get_barrier_semaphore()
     for k in range(1, n_feat):
         pl.semaphore_signal(barrier, 1, device_id={"feat": lax.rem(me + k, n_feat)}, device_id_type=MESH)
-    for o in range(1, group):
-        pl.semaphore_signal(barrier, 1, device_id={"tok": x * group + lax.rem(j + o, group)}, device_id_type=MESH)
-    pl.semaphore_signal(barrier, 1, device_id={"tok": partner}, device_id_type=MESH)
-    pl.semaphore_wait(barrier, n_feat - 1 + group - 1 + 1)
+    for o in range(1, n_y):
+        dest = x * 2 * n_y + lax.rem(y + o, n_y) * 2 + core
+        pl.semaphore_signal(barrier, 1, device_id={"tok": dest}, device_id_type=MESH)
+    pl.semaphore_signal(barrier, 1, device_id={"tok": core_peer}, device_id_type=MESH)
+    pl.semaphore_signal(barrier, 1, device_id={"tok": x_peer}, device_id_type=MESH)
+    pl.semaphore_wait(barrier, n_feat - 1 + n_y - 1 + 2)
 
     def feat_copies(c):
         cols = pl.ds(c * w, w)
@@ -69,55 +74,67 @@
                 p, q, (((0,), (0,)), ((), ())), preferred_element_type=jnp.float32
             ) * scale
             for xx in range(2):
-                for m in range(group):
-                    r0 = (xx * group + m) * piece
-                    gbuf[m, xx, k] = g[r0:r0 + piece, :]
+                for yy in range(n_y):
+                    for cc in range(2):
+                        r0 = ((xx * n_y + yy) * 2 + cc) * piece
+                        gbuf[cc, yy, xx, k] = g[r0:r0 + piece, :]
             return carry
 
         lax.fori_loop(0, slots, gram_one, 0)
 
-        own = pltpu.make_async_copy(gbuf.at[j], sta.at[c, j], alocal.at[c])
-        own.start()
-        a_copies = []
-        for o in range(1, group):
-            dest = lax.rem(j + o, group)
+        cp0 = pltpu.make_async_remote_copy(
+            src_ref=gbuf.at[1 - core],
+            dst_ref=st0.at[c],
+            send_sem=send0.at[c],
+            recv_sem=recv0.at[c],
+            device_id={"tok": core_peer},
+            device_id_type=MESH,
+        )
+        cp0.start()
+        cp0.wait()
+        s1buf[...] = gbuf[core] + st0[c]
+
+        copies1 = []
+        for o in range(1, n_y):
+            dy = lax.rem(y + o, n_y)
             cp = pltpu.make_async_remote_copy(
-                src_ref=gbuf.at[dest],
-                dst_ref=sta.at[c, j],
-                send_sem=asend.at[c, o],
-                recv_sem=arecv.at[c, o],
-                device_id={"tok": x * group + dest},
+                src_ref=s1buf.at[dy],
+                dst_ref=st1.at[c, y],
+                send_sem=send1.at[c, o],
+                recv_sem=recv1.at[c, o],
+                device_id={"tok": x * 2 * n_y + dy * 2 + core},
                 device_id_type=MESH,
             )
             cp.start()
-            a_copies.append(cp)
-        own.wait()
-        for cp in a_copies:
+            copies1.append(cp)
+        for cp in copies1:
             cp.wait()
-        acc = sta[c, 0]
-        for m in range(1, group):
-            acc = acc + sta[c, m]
-        accbuf[...] = acc
-        bcp = pltpu.make_async_remote_copy(
-            src_ref=accbuf.at[1 - x],
-            dst_ref=stb.at[c],
-            send_sem=bsend.at[c],
-            recv_sem=brecv.at[c],
-            device_id={"tok": partner},
+        acc = s1buf[y]
+        for o in range(1, n_y):
+            acc = acc + st1[c, lax.rem(y + o, n_y)]
+        s2buf[...] = acc
+
+        cp2 = pltpu.make_async_remote_copy(
+            src_ref=s2buf.at[1 - x],
+            dst_ref=st2.at[c],
+            send_sem=send2.at[c],
+            recv_sem=recv2.at[c],
+            device_id={"tok": x_peer},
             device_id_type=MESH,
         )
-        bcp.start()
-        bcp.wait()
-        out_ref[:, :, pl.ds(c * w, w)] = accbuf[x] + stb[c]
+        cp2.start()
+        cp2.wait()
+        out_ref[:, :, pl.ds(c * w, w)] = s2buf[x] + st2[c]
 
 
 def fused(holder, rowblk, send, activations, n_feat, n_tok, scale):
     slots = holder.shape[0]
     tokens, width = send.shape[1], send.shape[2]
     w = width // CHUNKS
-    group = n_tok // 2
+    n_y = n_tok // 4
     piece = width // n_tok
     kernel = functools.partial(fused_kernel, n_feat, n_tok, CHUNKS, scale)
+    blk = (slots, piece, w)
     return pl.pallas_call(
         kernel,
         out_shape=jax.ShapeDtypeStruct((slots, piece, width), jnp.float32),
@@ -129,16 +146,19 @@
         ],
         out_specs=pl.BlockSpec(memory_space=pltpu.VMEM),
         scratch_shapes=[pltpu.VMEM((n_feat, tokens, w), send.dtype) for _ in range(CHUNKS)] + [
-            pltpu.VMEM((group, 2, slots, piece, w), jnp.float32),
-            pltpu.VMEM((CHUNKS, group, 2, slots, piece, w), jnp.float32),
-            pltpu.VMEM((CHUNKS, slots, piece, w), jnp.float32),
-            pltpu.VMEM((2, slots, piece, w), jnp.float32),
+            pltpu.VMEM((2, n_y, 2) + blk, jnp.float32),
+            pltpu.VMEM((CHUNKS, n_y, 2) + blk, jnp.float32),
+            pltpu.VMEM((n_y, 2) + blk, jnp.float32),
+            pltpu.VMEM((CHUNKS, n_y, 2) + blk, jnp.float32),
+            pltpu.VMEM((2,) + blk, jnp.float32),
+            pltpu.VMEM((CHUNKS,) + blk, jnp.float32),
             pltpu.SemaphoreType.DMA((CHUNKS, n_feat)),
             pltpu.SemaphoreType.DMA((CHUNKS, n_feat)),
             pltpu.SemaphoreType.DMA((CHUNKS,)),
-            pltpu.SemaphoreType.DMA((CHUNKS, group)),
-            pltpu.SemaphoreType.DMA((CHUNKS, group)),
-            pltpu.SemaphoreType.DMA((CHUNKS,)),
+            pltpu.SemaphoreType.DMA((CHUNKS,)),
+            pltpu.SemaphoreType.DMA((CHUNKS,)),
+            pltpu.SemaphoreType.DMA((CHUNKS, n_y)),
+            pltpu.SemaphoreType.DMA((CHUNKS, n_y)),
             pltpu.SemaphoreType.DMA((CHUNKS,)),
             pltpu.SemaphoreType.DMA((CHUNKS,)),
         ],

time: 283 us -> 267 us (0.943)
  the two profiles are of different devices: /device:TPU:69 before, /device:TPU:4 now
where the time goes in v6:
time: 267 us; the launch traced here: 266 us
  Pallas kernels  260 us (97%)
  local copies, waits for them, and re-layouts  4.55 us (2%)
    pallas_call x1, Pallas kernels, fused(): pl.pallas_call(kernel, out_shape=jax.ShapeDtypeStruct((slots, piece, widt...  243 us
    pallas_call x2, Pallas kernels, gather_blocks(): pl.pallas_call(gather_kernel, out_shape=jax.ShapeDtypeStruct((count, toke...  16.6 us

profile of v6, /device:TPU:4, one launch (start us, length us, event | category | flops | bytes accessed | tf_op | source)
XLA Modules:
  0.0 266.4 jit_solution(2680886983402776178)
XLA Ops:
  0.0 0.5 iota.3.index_ref
  0.5 0.7 compare_select_fusion
  1.2 0.8 copy.4
  2.0 1.0 scatter_custom_fusion
  3.0 0.1 copy.5
  3.1 0.1 reshape.3
  3.2 0.7 fusion.4.index_ref
  3.9 0.6 and_select_fusion
  4.5 4.5 %shard_map.38.act_ref = bf16[4,512,512]{2,1,0:T(8,128)(2,1)} custom-call(s32[4]{0:T(128)} %iota.3.index_ref, bf16[512,2048]{1,0:T(8,128)(2,1)} %src_ref.3), custom_call_target="tpu_custom_call" | custom-call | tf_op jit(solution)/shard_map/pallas_call | solution.py:178
  9.0 12.1 %shard_map.37.send_ref = bf16[16,512,512]{2,1,0:T(8,128)(2,1)} custom-call(s32[16]{0:T(128)} %fusion.4.index_ref, bf16[512,2048]{1,0:T(8,128)(2,1)} %src_ref.3), custom_call_target="tpu_custom_call" | custom-call | tf_op jit(solution)/shard_map/pallas_call | solution.py:178
  21.1 243.2 %shard_map.39 = f32[12,32,512]{2,1,0:T(8,128)} custom-call(s32[12]{0:T(128)} %get-tuple-element.6.holder_ref, s32[12]{0:T(128)} %get-tuple-element.5.rowblk_ref, bf16[16,512,512]{2,1,0:T(8,128)(2,1)} %shard_map.37.send_ref, bf16[4,512,512]{2,1,0:T(8,128)(2,1)} %shard_map.38.act_ref), custom_call_target="tpu_custom_call" | custom-call | tf_op jit(solution)/shard_map/pallas_call | solution.py:138
  264.3 2.1 copy.7
  (1 shorter events, 0.0 us)

commit v7 on v6

--- a/solution.py
+++ b/solution.py
@@ -13,12 +13,13 @@
 
 
 def fused_kernel(n_feat, n_tok, chunks, scale,
-                 holder_ref, rowblk_ref, send_ref, act_ref, out_ref, *scratch):
+                 holder_ref, rowblk_ref, picked_ref, act_hbm, out_ref, *scratch):
     recv = scratch[:chunks]
-    (gbuf, st0, s1buf, st1, s2buf, st2,
+    (act_ref, send_ref, gbuf, st0, s1buf, st1, s2buf, st2, panel_sem,
      fsend, frecv, flocal, send0, recv0, send1, recv1, send2, recv2) = scratch[chunks:]
     slots = holder_ref.shape[0]
     tokens, width = send_ref.shape[1], send_ref.shape[2]
+    panel_blocks = act_ref.shape[0]
     w = width // chunks
     n_y = n_tok // 4
     piece = width // n_tok
@@ -39,6 +40,17 @@
     pl.semaphore_signal(barrier, 1, device_id={"tok": core_peer}, device_id_type=MESH)
     pl.semaphore_signal(barrier, 1, device_id={"tok": x_peer}, device_id_type=MESH)
     pl.semaphore_wait(barrier, n_feat - 1 + n_y - 1 + 2)
+
+    panel = [
+        pltpu.make_async_copy(act_hbm.at[:, pl.ds(b * width, width)], act_ref.at[b], panel_sem.at[b])
+        for b in range(panel_blocks)
+    ]
+    for cp in panel:
+        cp.start()
+    for cp in panel:
+        cp.wait()
+    for p in range(n_feat):
+        send_ref[p] = act_ref[picked_ref[p]]
 
     def feat_copies(c):
         cols = pl.ds(c * w, w)
@@ -127,9 +139,10 @@
         out_ref[:, :, pl.ds(c * w, w)] = s2buf[x] + st2[c]
 
 
-def fused(holder, rowblk, send, activations, n_feat, n_tok, scale):
+def fused(holder, rowblk, picked, activations, n_feat, n_tok, scale):
     slots = holder.shape[0]
-    tokens, width = send.shape[1], send.shape[2]
+    tokens, width = activations.shape[0], BLK
+    panel_blocks = activations.shape[1] // BLK
     w = width // CHUNKS
     n_y = n_tok // 4
     piece = width // n_tok
@@ -141,17 +154,20 @@
         in_specs=[
             pl.BlockSpec(memory_space=pltpu.SMEM),
             pl.BlockSpec(memory_space=pltpu.SMEM),
+            pl.BlockSpec(memory_space=pltpu.SMEM),
             pl.BlockSpec(memory_space=pl.ANY),
-            pl.BlockSpec(memory_space=pltpu.VMEM),
         ],
         out_specs=pl.BlockSpec(memory_space=pltpu.VMEM),
-        scratch_shapes=[pltpu.VMEM((n_feat, tokens, w), send.dtype) for _ in range(CHUNKS)] + [
+        scratch_shapes=[pltpu.VMEM((n_feat, tokens, w), activations.dtype) for _ in range(CHUNKS)] + [
+            pltpu.VMEM((panel_blocks, tokens, width), activations.dtype),
+            pltpu.VMEM((n_feat, tokens, width), activations.dtype),
             pltpu.VMEM((2, n_y, 2) + blk, jnp.float32),
             pltpu.VMEM((CHUNKS, n_y, 2) + blk, jnp.float32),
             pltpu.VMEM((n_y, 2) + blk, jnp.float32),
             pltpu.VMEM((CHUNKS, n_y, 2) + blk, jnp.float32),
             pltpu.VMEM((2,) + blk, jnp.float32),
             pltpu.VMEM((CHUNKS,) + blk, jnp.float32),
+            pltpu.SemaphoreType.DMA((panel_blocks,)),
             pltpu.SemaphoreType.DMA((CHUNKS, n_feat)),
             pltpu.SemaphoreType.DMA((CHUNKS, n_feat)),
             pltpu.SemaphoreType.DMA((CHUNKS,)),
@@ -165,26 +181,7 @@
         compiler_params=pltpu.CompilerParams(
             collective_id=0, has_side_effects=True, vmem_limit_bytes=60 * 1024 * 1024
         ),
-    )(holder, rowblk, send, activations)
-
-
-def gather_kernel(index_ref, src_ref, dst_ref):
-    dst_ref[0] = src_ref[...]
-
-
-def gather_blocks(activations, index):
-    tokens = activations.shape[0]
-    count = index.shape[0]
-    return pl.pallas_call(
-        gather_kernel,
-        out_shape=jax.ShapeDtypeStruct((count, tokens, BLK), activations.dtype),
-        grid_spec=pltpu.PrefetchScalarGridSpec(
-            num_scalar_prefetch=1,
-            grid=(count,),
-            in_specs=[pl.BlockSpec((tokens, BLK), lambda p, index_ref: (0, index_ref[p]))],
-            out_specs=pl.BlockSpec((1, tokens, BLK), lambda p, index_ref: (p, 0, 0)),
-        ),
-    )(index, activations)
+    )(holder, rowblk, picked, activations)
 
 
 def body(activations, pattern, block_slot):
@@ -203,10 +200,8 @@
     picked = jnp.sum(jnp.where(holder == my_index, local_column, 0), axis=1)
     my_pairs = lax.dynamic_index_in_dim(pairs, my_index, 0, keepdims=False)
     my_holder = my_pairs[:, 1] // panel_blocks
-    send = gather_blocks(activations, picked)
     rowblk = my_pairs[:, 0] % panel_blocks
-    blocks_local = gather_blocks(activations, jnp.arange(panel_blocks, dtype=jnp.int32))
-    out = fused(my_holder, rowblk, send, blocks_local, feat_count, tok_count, scale)
+    out = fused(my_holder, rowblk, picked, activations, feat_count, tok_count, scale)
     return out.transpose(1, 0, 2)
 
 

time: 267 us -> 256 us (0.959)
  the two profiles are of different devices: /device:TPU:4 before, /device:TPU:69 now
where the time goes in v7:
time: 256 us; the launch traced here: 254 us
  Pallas kernels  248 us (97%)
  local copies, waits for them, and re-layouts  4.06 us (2%)
    pallas_call x1, Pallas kernels, fused(): pl.pallas_call(kernel, out_shape=jax.ShapeDtypeStruct((slots, piece, widt...  248 us

profile of v7, /device:TPU:69, one launch (start us, length us, event | category | flops | bytes accessed | tf_op | source)
XLA Modules:
  0.0 253.5 jit_solution(2370336594967550716)
XLA Ops:
  0.0 0.7 compare_select_fusion
  0.7 0.8 copy.4
  1.5 1.0 scatter_custom_fusion
  2.5 0.1 copy.5
  2.6 0.1 reshape.3
  2.7 0.6 fusion.4.picked_ref
  3.3 0.6 and_select_fusion
  3.9 247.6 %shard_map.37 = f32[12,32,512]{2,1,0:T(8,128)} custom-call(s32[12]{0:T(128)} %get-tuple-element.6.holder_ref, s32[12]{0:T(128)} %get-tuple-element.5.rowblk_ref, s32[16]{0:T(128)} %fusion.4.picked_ref, bf16[512,2048]{1,0:T(8,128)(2,1)} %act_hbm.1), custom_call_target="tpu_custom_call" | custom-call | tf_op jit(solution)/shard_map/pallas_call | solution.py:151
  251.5 2.1 copy.7
  (1 shorter events, 0.0 us)

commit v8 on v7

--- a/solution.py
+++ b/solution.py
@@ -68,15 +68,17 @@
             ))
         return copies
 
-    pending = feat_copies(0)
-    for cp in pending:
-        cp.start()
+    in_flight = []
+    for c in range(min(2, chunks)):
+        in_flight.append(feat_copies(c))
+        for cp in in_flight[-1]:
+            cp.start()
     for c in range(chunks):
-        for cp in pending:
+        for cp in in_flight[c]:
             cp.wait()
-        if c + 1 < chunks:
-            pending = feat_copies(c + 1)
-            for cp in pending:
+        if c + 2 < chunks:
+            in_flight.append(feat_copies(c + 2))
+            for cp in in_flight[-1]:
                 cp.start()
 
         def gram_one(k, carry):

time: 256 us -> 238 us (0.930)
  Pallas kernels: 248 us -> 231 us
    pallas_call x1, Pallas kernels: 248 us -> 231 us  [fused(): pl.pallas_call(kernel, out_shape=jax.ShapeDtypeStruct((slots, piece, widt...]
where the time goes in v8:
time: 238 us; the launch traced here: 237 us
  Pallas kernels  231 us (97%)
  local copies, waits for them, and re-layouts  4.06 us (2%)
    pallas_call x1, Pallas kernels, fused(): pl.pallas_call(kernel, out_shape=jax.ShapeDtypeStruct((slots, piece, widt...  231 us

profile of v8, /device:TPU:69, one launch (start us, length us, event | category | flops | bytes accessed | tf_op | source)
XLA Modules:
  0.0 236.8 jit_solution(8957388013990122135)
XLA Ops:
  0.0 0.7 compare_select_fusion
  0.7 0.8 copy.4
  1.5 1.0 scatter_custom_fusion
  2.5 0.1 copy.5
  2.6 0.1 reshape.3
  2.7 0.6 fusion.4.picked_ref
  3.3 0.6 and_select_fusion
  3.9 230.8 %shard_map.37 = f32[12,32,512]{2,1,0:T(8,128)} custom-call(s32[12]{0:T(128)} %get-tuple-element.6.holder_ref, s32[12]{0:T(128)} %get-tuple-element.5.rowblk_ref, s32[16]{0:T(128)} %fusion.4.picked_ref, bf16[512,2048]{1,0:T(8,128)(2,1)} %act_hbm.1), custom_call_target="tpu_custom_call" | custom-call | tf_op jit(solution)/shard_map/pallas_call | solution.py:153
  234.7 2.1 copy.7
  (1 shorter events, 0.0 us)

commit v9 on v8

--- a/solution.py
+++ b/solution.py
@@ -9,6 +9,7 @@
 
 BLK = 512
 CHUNKS = 4
+DEPTH = 4
 MESH = pl.DeviceIdType.MESH
 
 
@@ -69,15 +70,15 @@
         return copies
 
     in_flight = []
-    for c in range(min(2, chunks)):
+    for c in range(min(DEPTH, chunks)):
         in_flight.append(feat_copies(c))
         for cp in in_flight[-1]:
             cp.start()
     for c in range(chunks):
         for cp in in_flight[c]:
             cp.wait()
-        if c + 2 < chunks:
-            in_flight.append(feat_copies(c + 2))
+        if c + DEPTH < chunks:
+            in_flight.append(feat_copies(c + DEPTH))
             for cp in in_flight[-1]:
                 cp.start()
 

time: 238 us -> 238 us (level)
  no operation moved by 1% of the time
where the time goes in v9:
time: 238 us; the launch traced here: 237 us
  Pallas kernels  231 us (97%)
  local copies, waits for them, and re-layouts  4.06 us (2%)
    pallas_call x1, Pallas kernels, fused(): pl.pallas_call(kernel, out_shape=jax.ShapeDtypeStruct((slots, piece, widt...  231 us

profile of v9, /device:TPU:69, one launch (start us, length us, event | category | flops | bytes accessed | tf_op | source)
XLA Modules:
  0.0 236.9 jit_solution(7370431132529053536)
XLA Ops:
  0.0 0.7 compare_select_fusion
  0.7 0.8 copy.4
  1.5 1.0 scatter_custom_fusion
  2.5 0.1 copy.5
  2.6 0.1 reshape.3
  2.7 0.6 fusion.4.picked_ref
  3.3 0.6 and_select_fusion
  3.9 230.9 %shard_map.37 = f32[12,32,512]{2,1,0:T(8,128)} custom-call(s32[12]{0:T(128)} %get-tuple-element.6.holder_ref, s32[12]{0:T(128)} %get-tuple-element.5.rowblk_ref, s32[16]{0:T(128)} %fusion.4.picked_ref, bf16[512,2048]{1,0:T(8,128)(2,1)} %act_hbm.1), custom_call_target="tpu_custom_call" | custom-call | tf_op jit(solution)/shard_map/pallas_call | solution.py:154
  234.8 2.1 copy.7
  (1 shorter events, 0.0 us)

commit v10 on v8

--- a/solution.py
+++ b/solution.py
@@ -49,8 +49,6 @@
         cp.start()
     for cp in panel:
         cp.wait()
-    for p in range(n_feat):
-        send_ref[p] = act_ref[picked_ref[p]]
 
     def feat_copies(c):
         cols = pl.ds(c * w, w)
@@ -68,11 +66,12 @@
             ))
         return copies
 
-    in_flight = []
-    for c in range(min(2, chunks)):
-        in_flight.append(feat_copies(c))
-        for cp in in_flight[-1]:
-            cp.start()
+    in_flight = [feat_copies(c) for c in range(min(2, chunks))]
+    for k in list(range(1, n_feat)) + [0]:
+        peer = lax.rem(me + k, n_feat)
+        send_ref[peer] = act_ref[picked_ref[peer]]
+        for copies in in_flight:
+            copies[k].start()
     for c in range(chunks):
         for cp in in_flight[c]:
             cp.wait()

time: 238 us -> 263 us (1.11)
  Pallas kernels: 231 us -> 256 us
    pallas_call x1, Pallas kernels: 231 us -> 256 us  [fused(): pl.pallas_call(kernel, out_shape=jax.ShapeDtypeStruct((slots, piece, widt...]
where the time goes in v10:
time: 263 us; the launch traced here: 262 us
  Pallas kernels  256 us (97%)
  local copies, waits for them, and re-layouts  4.06 us (2%)
    pallas_call x1, Pallas kernels, fused(): pl.pallas_call(kernel, out_shape=jax.ShapeDtypeStruct((slots, piece, widt...  256 us

profile of v10, /device:TPU:69, one launch (start us, length us, event | category | flops | bytes accessed | tf_op | source)
XLA Modules:
  0.0 262.1 jit_solution(8396653355008814568)
XLA Ops:
  0.0 0.7 compare_select_fusion
  0.7 0.8 copy.4
  1.5 1.0 scatter_custom_fusion
  2.5 0.1 copy.5
  2.6 0.1 reshape.3
  2.7 0.6 fusion.4.picked_ref
  3.3 0.6 and_select_fusion
  3.9 256.1 %shard_map.37 = f32[12,32,512]{2,1,0:T(8,128)} custom-call(s32[12]{0:T(128)} %get-tuple-element.6.holder_ref, s32[12]{0:T(128)} %get-tuple-element.5.rowblk_ref, s32[16]{0:T(128)} %fusion.4.picked_ref, bf16[512,2048]{1,0:T(8,128)(2,1)} %act_hbm.1), custom_call_target="tpu_custom_call" | custom-call | tf_op jit(solution)/shard_map/pallas_call | solution.py:152
  260.0 2.1 copy.7
  (1 shorter events, 0.0 us)

commit v11 on v8

--- a/solution.py
+++ b/solution.py
@@ -15,8 +15,8 @@
 def fused_kernel(n_feat, n_tok, chunks, scale,
                  holder_ref, rowblk_ref, picked_ref, act_hbm, out_ref, *scratch):
     recv = scratch[:chunks]
-    (act_ref, send_ref, gbuf, st0, s1buf, st1, s2buf, st2, panel_sem,
-     fsend, frecv, flocal, send0, recv0, send1, recv1, send2, recv2) = scratch[chunks:]
+    (act_ref, send_ref, gbuf, st0, s1buf, st1, s2buf, st2, stz, panel_sem,
+     fsend, frecv, flocal, send0, recv0, send1, recv1, send2, recv2, zsend, zrecv) = scratch[chunks:]
     slots = holder_ref.shape[0]
     tokens, width = send_ref.shape[1], send_ref.shape[2]
     panel_blocks = act_ref.shape[0]
@@ -34,12 +34,9 @@
     barrier = pltpu.get_barrier_semaphore()
     for k in range(1, n_feat):
         pl.semaphore_signal(barrier, 1, device_id={"feat": lax.rem(me + k, n_feat)}, device_id_type=MESH)
-    for o in range(1, n_y):
-        dest = x * 2 * n_y + lax.rem(y + o, n_y) * 2 + core
-        pl.semaphore_signal(barrier, 1, device_id={"tok": dest}, device_id_type=MESH)
-    pl.semaphore_signal(barrier, 1, device_id={"tok": core_peer}, device_id_type=MESH)
-    pl.semaphore_signal(barrier, 1, device_id={"tok": x_peer}, device_id_type=MESH)
-    pl.semaphore_wait(barrier, n_feat - 1 + n_y - 1 + 2)
+    for o in range(1, n_tok):
+        pl.semaphore_signal(barrier, 1, device_id={"tok": lax.rem(t + o, n_tok)}, device_id_type=MESH)
+    pl.semaphore_wait(barrier, n_feat - 1 + n_tok - 1)
 
     panel = [
         pltpu.make_async_copy(act_hbm.at[:, pl.ds(b * width, width)], act_ref.at[b], panel_sem.at[b])
@@ -95,6 +92,28 @@
             return carry
 
         lax.fori_loop(0, slots, gram_one, 0)
+
+        if c == chunks - 1:
+            last = []
+            for o in range(1, n_tok):
+                dest = lax.rem(t + o, n_tok)
+                cp = pltpu.make_async_remote_copy(
+                    src_ref=gbuf.at[dest % 2, (dest // 2) % n_y, dest // (2 * n_y)],
+                    dst_ref=stz.at[o],
+                    send_sem=zsend.at[o],
+                    recv_sem=zrecv.at[o],
+                    device_id={"tok": dest},
+                    device_id_type=MESH,
+                )
+                cp.start()
+                last.append(cp)
+            for cp in last:
+                cp.wait()
+            acc = gbuf[core, y, x]
+            for o in range(1, n_tok):
+                acc = acc + stz[o]
+            out_ref[:, :, pl.ds(c * w, w)] = acc
+            continue
 
         cp0 = pltpu.make_async_remote_copy(
             src_ref=gbuf.at[1 - core],
@@ -169,6 +188,7 @@
             pltpu.VMEM((CHUNKS, n_y, 2) + blk, jnp.float32),
             pltpu.VMEM((2,) + blk, jnp.float32),
             pltpu.VMEM((CHUNKS,) + blk, jnp.float32),
+            pltpu.VMEM((n_tok,) + blk, jnp.float32),
             pltpu.SemaphoreType.DMA((panel_blocks,)),
             pltpu.SemaphoreType.DMA((CHUNKS, n_feat)),
             pltpu.SemaphoreType.DMA((CHUNKS, n_feat)),
@@ -179,6 +199,8 @@
             pltpu.SemaphoreType.DMA((CHUNKS, n_y)),
             pltpu.SemaphoreType.DMA((CHUNKS,)),
             pltpu.SemaphoreType.DMA((CHUNKS,)),
+            pltpu.SemaphoreType.DMA((n_tok,)),
+            pltpu.SemaphoreType.DMA((n_tok,)),
         ],
         compiler_params=pltpu.CompilerParams(
             collective_id=0, has_side_effects=True, vmem_limit_bytes=60 * 1024 * 1024

time: 238 us -> 257 us (1.080)
  Pallas kernels: 231 us -> 247 us
    pallas_call x1, Pallas kernels: 231 us -> 247 us  [fused(): pl.pallas_call(kernel, out_shape=jax.ShapeDtypeStruct((slots, piece, widt...]
where the time goes in v11:
time: 257 us; the launch traced here: 253 us
  Pallas kernels  247 us (96%)
  local copies, waits for them, and re-layouts  4.06 us (2%)
    pallas_call x1, Pallas kernels, fused(): pl.pallas_call(kernel, out_shape=jax.ShapeDtypeStruct((slots, piece, widt...  247 us

profile of v11, /device:TPU:69, one launch (start us, length us, event | category | flops | bytes accessed | tf_op | source)
XLA Modules:
  0.0 253.3 jit_solution(2800128502816819237)
XLA Ops:
  0.0 0.7 compare_select_fusion
  0.7 0.8 copy.4
  1.5 1.0 scatter_custom_fusion
  2.5 0.1 copy.5
  2.6 0.1 reshape.3
  2.7 0.6 fusion.4.picked_ref
  3.3 0.6 and_select_fusion
  3.9 247.3 %shard_map.37 = f32[12,32,512]{2,1,0:T(8,128)} custom-call(s32[12]{0:T(128)} %get-tuple-element.6.holder_ref, s32[12]{0:T(128)} %get-tuple-element.5.rowblk_ref, s32[16]{0:T(128)} %fusion.4.picked_ref, bf16[512,2048]{1,0:T(8,128)(2,1)} %act_hbm.1), custom_call_target="tpu_custom_call" | custom-call | tf_op jit(solution)/shard_map/pallas_call | solution.py:172
  251.2 2.1 copy.7
  (1 shorter events, 0.0 us)

commit v12 on v8

--- a/solution.py
+++ b/solution.py
@@ -39,7 +39,6 @@
         pl.semaphore_signal(barrier, 1, device_id={"tok": dest}, device_id_type=MESH)
     pl.semaphore_signal(barrier, 1, device_id={"tok": core_peer}, device_id_type=MESH)
     pl.semaphore_signal(barrier, 1, device_id={"tok": x_peer}, device_id_type=MESH)
-    pl.semaphore_wait(barrier, n_feat - 1 + n_y - 1 + 2)
 
     panel = [
         pltpu.make_async_copy(act_hbm.at[:, pl.ds(b * width, width)], act_ref.at[b], panel_sem.at[b])
@@ -51,6 +50,8 @@
         cp.wait()
     for p in range(n_feat):
         send_ref[p] = act_ref[picked_ref[p]]
+
+    pl.semaphore_wait(barrier, n_feat - 1 + n_y - 1 + 2)
 
     def feat_copies(c):
         cols = pl.ds(c * w, w)

time: 238 us -> 236 us (level)
  no operation moved by 1% of the time
where the time goes in v12:
time: 236 us; the launch traced here: 235 us
  Pallas kernels  229 us (97%)
  local copies, waits for them, and re-layouts  4.06 us (2%)
    pallas_call x1, Pallas kernels, fused(): pl.pallas_call(kernel, out_shape=jax.ShapeDtypeStruct((slots, piece, widt...  229 us

profile of v12, /device:TPU:69, one launch (start us, length us, event | category | flops | bytes accessed | tf_op | source)
XLA Modules:
  0.0 234.7 jit_solution(1881463253033385553)
XLA Ops:
  0.0 0.7 compare_select_fusion
  0.7 0.8 copy.4
  1.5 1.0 scatter_custom_fusion
  2.5 0.1 copy.5
  2.6 0.1 reshape.3
  2.7 0.6 fusion.4.picked_ref
  3.3 0.6 and_select_fusion
  3.9 228.7 %shard_map.37 = f32[12,32,512]{2,1,0:T(8,128)} custom-call(s32[12]{0:T(128)} %get-tuple-element.6.holder_ref, s32[12]{0:T(128)} %get-tuple-element.5.rowblk_ref, s32[16]{0:T(128)} %fusion.4.picked_ref, bf16[512,2048]{1,0:T(8,128)(2,1)} %act_hbm.1), custom_call_target="tpu_custom_call" | custom-call | tf_op jit(solution)/shard_map/pallas_call | solution.py:154
  232.6 2.1 copy.7
  (1 shorter events, 0.0 us)

commit v13 on v12

--- a/solution.py
+++ b/solution.py
@@ -15,7 +15,7 @@
 def fused_kernel(n_feat, n_tok, chunks, scale,
                  holder_ref, rowblk_ref, picked_ref, act_hbm, out_ref, *scratch):
     recv = scratch[:chunks]
-    (act_ref, send_ref, gbuf, st0, s1buf, st1, s2buf, st2, panel_sem,
+    (act_ref, actt_ref, send_ref, gbuf, st0, s1buf, st1, s2buf, st2, panel_sem,
      fsend, frecv, flocal, send0, recv0, send1, recv1, send2, recv2) = scratch[chunks:]
     slots = holder_ref.shape[0]
     tokens, width = send_ref.shape[1], send_ref.shape[2]
@@ -50,6 +50,8 @@
         cp.wait()
     for p in range(n_feat):
         send_ref[p] = act_ref[picked_ref[p]]
+    for b in range(panel_blocks):
+        actt_ref[b] = act_ref[b].T
 
     pl.semaphore_wait(barrier, n_feat - 1 + n_y - 1 + 2)
 
@@ -84,10 +86,8 @@
 
         def gram_one(k, carry):
             q = recv[c][holder_ref[k]]
-            p = act_ref[rowblk_ref[k]]
-            g = lax.dot_general(
-                p, q, (((0,), (0,)), ((), ())), preferred_element_type=jnp.float32
-            ) * scale
+            p = actt_ref[rowblk_ref[k]]
+            g = jnp.dot(p, q, preferred_element_type=jnp.float32) * scale
             for xx in range(2):
                 for yy in range(n_y):
                     for cc in range(2):
@@ -163,6 +163,7 @@
         out_specs=pl.BlockSpec(memory_space=pltpu.VMEM),
         scratch_shapes=[pltpu.VMEM((n_feat, tokens, w), activations.dtype) for _ in range(CHUNKS)] + [
             pltpu.VMEM((panel_blocks, tokens, width), activations.dtype),
+            pltpu.VMEM((panel_blocks, width, tokens), activations.dtype),
             pltpu.VMEM((n_feat, tokens, width), activations.dtype),
             pltpu.VMEM((2, n_y, 2) + blk, jnp.float32),
             pltpu.VMEM((CHUNKS, n_y, 2) + blk, jnp.float32),

time: 236 us -> 236 us (level)
  no operation moved by 1% of the time
where the time goes in v13:
time: 236 us; the launch traced here: 234 us
  Pallas kernels  228 us (97%)
  local copies, waits for them, and re-layouts  4.06 us (2%)
    pallas_call x1, Pallas kernels, fused(): pl.pallas_call(kernel, out_shape=jax.ShapeDtypeStruct((slots, piece, widt...  228 us

profile of v13, /device:TPU:69, one launch (start us, length us, event | category | flops | bytes accessed | tf_op | source)
XLA Modules:
  0.0 234.1 jit_solution(18382002810708751374)
XLA Ops:
  0.0 0.7 compare_select_fusion
  0.7 0.8 copy.4
  1.5 1.0 scatter_custom_fusion
  2.5 0.1 copy.5
  2.6 0.1 reshape.3
  2.7 0.6 fusion.4.picked_ref
  3.3 0.6 and_select_fusion
  3.9 228.1 %shard_map.37 = f32[12,32,512]{2,1,0:T(8,128)} custom-call(s32[12]{0:T(128)} %get-tuple-element.6.holder_ref, s32[12]{0:T(128)} %get-tuple-element.5.rowblk_ref, s32[16]{0:T(128)} %fusion.4.picked_ref, bf16[512,2048]{1,0:T(8,128)(2,1)} %act_hbm.1), custom_call_target="tpu_custom_call" | custom-call | tf_op jit(solution)/shard_map/pallas_call | solution.py:154
  232.0 2.1 copy.7
  (1 shorter events, 0.0 us)

commit v14 on v12

--- a/solution.py
+++ b/solution.py
@@ -16,7 +16,8 @@
                  holder_ref, rowblk_ref, picked_ref, act_hbm, out_ref, *scratch):
     recv = scratch[:chunks]
     (act_ref, send_ref, gbuf, st0, s1buf, st1, s2buf, st2, panel_sem,
-     fsend, frecv, flocal, send0, recv0, send1, recv1, send2, recv2) = scratch[chunks:]
+     fsend, frecv, flocal, send0, recv0, send1, recv1, send2, recv2,
+     bxbuf, bsum, bybuf, bsem, bysend, byrecv) = scratch[chunks:]
     slots = holder_ref.shape[0]
     tokens, width = send_ref.shape[1], send_ref.shape[2]
     panel_blocks = act_ref.shape[0]
@@ -69,6 +70,63 @@
             ))
         return copies
 
+    def reduce_last(c):
+        h = slots // 2
+        cols = pl.ds(c * w, w)
+        cp0 = pltpu.make_async_remote_copy(
+            src_ref=gbuf.at[1 - core], dst_ref=st0.at[c], send_sem=send0.at[c],
+            recv_sem=recv0.at[c], device_id={"tok": core_peer}, device_id_type=MESH,
+        )
+        cp0.start()
+        cp0.wait()
+        s1buf[...] = gbuf[core] + st0[c]
+        a_y = []
+        for o in range(1, n_y):
+            dy = lax.rem(y + o, n_y)
+            cp = pltpu.make_async_remote_copy(
+                src_ref=s1buf.at[dy, :, pl.ds(0, h)], dst_ref=st1.at[c, y, :, pl.ds(0, h)],
+                send_sem=send1.at[c, o], recv_sem=recv1.at[c, o],
+                device_id={"tok": x * 2 * n_y + dy * 2 + core}, device_id_type=MESH,
+            )
+            cp.start()
+            a_y.append(cp)
+        b_x = pltpu.make_async_remote_copy(
+            src_ref=s1buf.at[:, 1 - x, pl.ds(h, slots - h)], dst_ref=bxbuf,
+            send_sem=bsem.at[0], recv_sem=bsem.at[1], device_id={"tok": x_peer}, device_id_type=MESH,
+        )
+        b_x.start()
+        b_x.wait()
+        bsum[...] = s1buf[:, x, h:] + bxbuf[...]
+        b_y = []
+        for o in range(1, n_y):
+            dy = lax.rem(y + o, n_y)
+            cp = pltpu.make_async_remote_copy(
+                src_ref=bsum.at[dy], dst_ref=bybuf.at[y],
+                send_sem=bysend.at[o], recv_sem=byrecv.at[o],
+                device_id={"tok": x * 2 * n_y + dy * 2 + core}, device_id_type=MESH,
+            )
+            cp.start()
+            b_y.append(cp)
+        for cp in a_y:
+            cp.wait()
+        acc = s1buf[y, :, :h]
+        for o in range(1, n_y):
+            acc = acc + st1[c, lax.rem(y + o, n_y), :, :h]
+        s2buf[:, :h] = acc
+        a_x = pltpu.make_async_remote_copy(
+            src_ref=s2buf.at[1 - x, pl.ds(0, h)], dst_ref=st2.at[c, pl.ds(0, h)],
+            send_sem=send2.at[c], recv_sem=recv2.at[c], device_id={"tok": x_peer}, device_id_type=MESH,
+        )
+        a_x.start()
+        for cp in b_y:
+            cp.wait()
+        accb = bsum[y]
+        for o in range(1, n_y):
+            accb = accb + bybuf[lax.rem(y + o, n_y)]
+        out_ref[h:, :, cols] = accb
+        a_x.wait()
+        out_ref[:h, :, cols] = s2buf[x, :h] + st2[c, :h]
+
     in_flight = []
     for c in range(min(2, chunks)):
         in_flight.append(feat_copies(c))
@@ -96,6 +154,10 @@
             return carry
 
         lax.fori_loop(0, slots, gram_one, 0)
+
+        if c == chunks - 1 and slots > 1:
+            reduce_last(c)
+            continue
 
         cp0 = pltpu.make_async_remote_copy(
             src_ref=gbuf.at[1 - core],
@@ -180,6 +242,12 @@
             pltpu.SemaphoreType.DMA((CHUNKS, n_y)),
             pltpu.SemaphoreType.DMA((CHUNKS,)),
             pltpu.SemaphoreType.DMA((CHUNKS,)),
+            pltpu.VMEM((n_y, slots - slots // 2, piece, w), jnp.float32),
+            pltpu.VMEM((n_y, slots - slots // 2, piece, w), jnp.float32),
+            pltpu.VMEM((n_y, slots - slots // 2, piece, w), jnp.float32),
+            pltpu.SemaphoreType.DMA((2,)),
+            pltpu.SemaphoreType.DMA((n_y,)),
+            pltpu.SemaphoreType.DMA((n_y,)),
         ],
         compiler_params=pltpu.CompilerParams(
             collective_id=0, has_side_effects=True, vmem_limit_bytes=60 * 1024 * 1024

time: 236 us -> 228 us (0.966)
  Pallas kernels: 229 us -> 220 us
    pallas_call x1, Pallas kernels: 229 us -> 220 us  [fused(): pl.pallas_call(kernel, out_shape=jax.ShapeDtypeStruct((slots, piece, widt...]
where the time goes in v14:
time: 228 us; the launch traced here: 226 us
  Pallas kernels  220 us (96%)
  local copies, waits for them, and re-layouts  4.06 us (2%)
    pallas_call x1, Pallas kernels, fused(): pl.pallas_call(kernel, out_shape=jax.ShapeDtypeStruct((slots, piece, widt...  220 us

profile of v14, /device:TPU:69, one launch (start us, length us, event | category | flops | bytes accessed | tf_op | source)
XLA Modules:
  0.0 226.3 jit_solution(9633173910296192745)
XLA Ops:
  0.0 0.7 compare_select_fusion
  0.7 0.8 copy.4
  1.5 1.0 scatter_custom_fusion
  2.5 0.1 copy.5
  2.6 0.1 reshape.3
  2.7 0.6 fusion.4.picked_ref
  3.3 0.6 and_select_fusion
  3.9 220.4 %shard_map.37 = f32[12,32,512]{2,1,0:T(8,128)} custom-call(s32[12]{0:T(128)} %get-tuple-element.6.holder_ref, s32[12]{0:T(128)} %get-tuple-element.5.rowblk_ref, s32[16]{0:T(128)} %fusion.4.picked_ref, bf16[512,2048]{1,0:T(8,128)(2,1)} %act_hbm.1), custom_call_target="tpu_custom_call" | custom-call | tf_op jit(solution)/shard_map/pallas_call | solution.py:216
  224.3 2.1 copy.7
  (1 shorter events, 0.0 us)

commit v15 on v14

--- a/solution.py
+++ b/solution.py
@@ -73,13 +73,19 @@
     def reduce_last(c):
         h = slots // 2
         cols = pl.ds(c * w, w)
-        cp0 = pltpu.make_async_remote_copy(
-            src_ref=gbuf.at[1 - core], dst_ref=st0.at[c], send_sem=send0.at[c],
-            recv_sem=recv0.at[c], device_id={"tok": core_peer}, device_id_type=MESH,
-        )
-        cp0.start()
-        cp0.wait()
-        s1buf[...] = gbuf[core] + st0[c]
+        cp0a = pltpu.make_async_remote_copy(
+            src_ref=gbuf.at[1 - core, :, :, pl.ds(0, h)], dst_ref=st0.at[c, :, :, pl.ds(0, h)],
+            send_sem=send0.at[c], recv_sem=recv0.at[c], device_id={"tok": core_peer}, device_id_type=MESH,
+        )
+        cp0b = pltpu.make_async_remote_copy(
+            src_ref=gbuf.at[1 - core, :, :, pl.ds(h, slots - h)],
+            dst_ref=st0.at[c, :, :, pl.ds(h, slots - h)],
+            send_sem=bsem.at[2], recv_sem=bsem.at[3], device_id={"tok": core_peer}, device_id_type=MESH,
+        )
+        cp0a.start()
+        cp0b.start()
+        cp0a.wait()
+        s1buf[:, :, :h] = gbuf[core, :, :, :h] + st0[c, :, :, :h]
         a_y = []
         for o in range(1, n_y):
             dy = lax.rem(y + o, n_y)
@@ -90,6 +96,8 @@
             )
             cp.start()
             a_y.append(cp)
+        cp0b.wait()
+        s1buf[:, :, h:] = gbuf[core, :, :, h:] + st0[c, :, :, h:]
         b_x = pltpu.make_async_remote_copy(
             src_ref=s1buf.at[:, 1 - x, pl.ds(h, slots - h)], dst_ref=bxbuf,
             send_sem=bsem.at[0], recv_sem=bsem.at[1], device_id={"tok": x_peer}, device_id_type=MESH,
@@ -245,7 +253,7 @@
             pltpu.VMEM((n_y, slots - slots // 2, piece, w), jnp.float32),
             pltpu.VMEM((n_y, slots - slots // 2, piece, w), jnp.float32),
             pltpu.VMEM((n_y, slots - slots // 2, piece, w), jnp.float32),
-            pltpu.SemaphoreType.DMA((2,)),
+            pltpu.SemaphoreType.DMA((4,)),
             pltpu.SemaphoreType.DMA((n_y,)),
             pltpu.SemaphoreType.DMA((n_y,)),
         ],

time: 228 us -> 228 us (level)
  no operation moved by 1% of the time
where the time goes in v15:
time: 228 us; the launch traced here: 226 us
  Pallas kernels  220 us (96%)
  local copies, waits for them, and re-layouts  4.06 us (2%)
    pallas_call x1, Pallas kernels, fused(): pl.pallas_call(kernel, out_shape=jax.ShapeDtypeStruct((slots, piece, widt...  220 us

profile of v15, /device:TPU:69, one launch (start us, length us, event | category | flops | bytes accessed | tf_op | source)
XLA Modules:
  0.0 226.3 jit_solution(8923952856043267216)
XLA Ops:
  0.0 0.7 compare_select_fusion
  0.7 0.8 copy.4
  1.5 1.0 scatter_custom_fusion
  2.5 0.1 copy.5
  2.6 0.1 reshape.3
  2.7 0.6 fusion.4.picked_ref
  3.3 0.6 and_select_fusion
  3.9 220.3 %shard_map.37 = f32[12,32,512]{2,1,0:T(8,128)} custom-call(s32[12]{0:T(128)} %get-tuple-element.6.holder_ref, s32[12]{0:T(128)} %get-tuple-element.5.rowblk_ref, s32[16]{0:T(128)} %fusion.4.picked_ref, bf16[512,2048]{1,0:T(8,128)(2,1)} %act_hbm.1), custom_call_target="tpu_custom_call" | custom-call | tf_op jit(solution)/shard_map/pallas_call | solution.py:224
  224.2 2.1 copy.7
  (1 shorter events, 0.0 us)

commit v16 on v14

--- a/solution.py
+++ b/solution.py
@@ -58,7 +58,7 @@
         cols = pl.ds(c * w, w)
         local = pltpu.make_async_copy(send_ref.at[me, :, cols], recv[c].at[me], flocal.at[c])
         copies = [local]
-        for k in range(1, n_feat):
+        for k in sorted(range(1, n_feat), key=lambda k: -min(k, n_feat - k)):
             peer = lax.rem(me + k, n_feat)
             copies.append(pltpu.make_async_remote_copy(
                 src_ref=send_ref.at[peer, :, cols],

time: 228 us -> 231 us (1.013); the launches traced: 226 us -> 227 us
  no operation moved by 1% of the time
where the time goes in v16:
time: 231 us; the launch traced here: 227 us
  Pallas kernels  221 us (96%)
  local copies, waits for them, and re-layouts  4.06 us (2%)
    pallas_call x1, Pallas kernels, fused(): pl.pallas_call(kernel, out_shape=jax.ShapeDtypeStruct((slots, piece, widt...  221 us

profile of v16, /device:TPU:69, one launch (start us, length us, event | category | flops | bytes accessed | tf_op | source)
XLA Modules:
  0.0 226.8 jit_solution(11711658026053354438)
XLA Ops:
  0.0 0.7 compare_select_fusion
  0.7 0.8 copy.4
  1.5 1.0 scatter_custom_fusion
  2.5 0.1 copy.5
  2.6 0.1 reshape.3
  2.7 0.6 fusion.4.picked_ref
  3.3 0.6 and_select_fusion
  3.9 220.8 %shard_map.37 = f32[12,32,512]{2,1,0:T(8,128)} custom-call(s32[12]{0:T(128)} %get-tuple-element.6.holder_ref, s32[12]{0:T(128)} %get-tuple-element.5.rowblk_ref, s32[16]{0:T(128)} %fusion.4.picked_ref, bf16[512,2048]{1,0:T(8,128)(2,1)} %act_hbm.1), custom_call_target="tpu_custom_call" | custom-call | tf_op jit(solution)/shard_map/pallas_call | solution.py:216
  224.8 2.1 copy.7
  (1 shorter events, 0.0 us)

commit v17 on v16

--- a/solution.py
+++ b/solution.py
@@ -58,7 +58,7 @@
         cols = pl.ds(c * w, w)
         local = pltpu.make_async_copy(send_ref.at[me, :, cols], recv[c].at[me], flocal.at[c])
         copies = [local]
-        for k in sorted(range(1, n_feat), key=lambda k: -min(k, n_feat - k)):
+        for k in sorted(range(1, n_feat), key=lambda k: min(k, n_feat - k)):
             peer = lax.rem(me + k, n_feat)
             copies.append(pltpu.make_async_remote_copy(
                 src_ref=send_ref.at[peer, :, cols],

time: 231 us -> 226 us (0.978)
  Pallas kernels: 221 us -> 217 us
    pallas_call x1, Pallas kernels: 221 us -> 217 us  [fused(): pl.pallas_call(kernel, out_shape=jax.ShapeDtypeStruct((slots, piece, widt...]
where the time goes in v17:
time: 226 us; the launch traced here: 223 us
  Pallas kernels  217 us (96%)
  local copies, waits for them, and re-layouts  4.06 us (2%)
    pallas_call x1, Pallas kernels, fused(): pl.pallas_call(kernel, out_shape=jax.ShapeDtypeStruct((slots, piece, widt...  217 us

profile of v17, /device:TPU:69, one launch (start us, length us, event | category | flops | bytes accessed | tf_op | source)
XLA Modules:
  0.0 223.3 jit_solution(16527871454486816688)
XLA Ops:
  0.0 0.7 compare_select_fusion
  0.7 0.8 copy.4
  1.5 1.0 scatter_custom_fusion
  2.5 0.1 copy.5
  2.6 0.1 reshape.3
  2.7 0.6 fusion.4.picked_ref
  3.3 0.6 and_select_fusion
  3.9 217.3 %shard_map.37 = f32[12,32,512]{2,1,0:T(8,128)} custom-call(s32[12]{0:T(128)} %get-tuple-element.6.holder_ref, s32[12]{0:T(128)} %get-tuple-element.5.rowblk_ref, s32[16]{0:T(128)} %fusion.4.picked_ref, bf16[512,2048]{1,0:T(8,128)(2,1)} %act_hbm.1), custom_call_target="tpu_custom_call" | custom-call | tf_op jit(solution)/shard_map/pallas_call | solution.py:216
  221.2 2.1 copy.7
  (1 shorter events, 0.0 us)

commit v18 on v17

--- a/solution.py
+++ b/solution.py
@@ -71,7 +71,7 @@
         return copies
 
     def reduce_last(c):
-        h = slots // 2
+        h = (slots * 5) // 12
         cols = pl.ds(c * w, w)
         cp0 = pltpu.make_async_remote_copy(
             src_ref=gbuf.at[1 - core], dst_ref=st0.at[c], send_sem=send0.at[c],
@@ -242,9 +242,9 @@
             pltpu.SemaphoreType.DMA((CHUNKS, n_y)),
             pltpu.SemaphoreType.DMA((CHUNKS,)),
             pltpu.SemaphoreType.DMA((CHUNKS,)),
-            pltpu.VMEM((n_y, slots - slots // 2, piece, w), jnp.float32),
-            pltpu.VMEM((n_y, slots - slots // 2, piece, w), jnp.float32),
-            pltpu.VMEM((n_y, slots - slots // 2, piece, w), jnp.float32),
+            pltpu.VMEM((n_y, slots - (slots * 5) // 12, piece, w), jnp.float32),
+            pltpu.VMEM((n_y, slots - (slots * 5) // 12, piece, w), jnp.float32),
+            pltpu.VMEM((n_y, slots - (slots * 5) // 12, piece, w), jnp.float32),
             pltpu.SemaphoreType.DMA((2,)),
             pltpu.SemaphoreType.DMA((n_y,)),
             pltpu.SemaphoreType.DMA((n_y,)),

time: 226 us -> 228 us (level)
  no operation moved by 1% of the time
where the time goes in v18:
time: 228 us; the launch traced here: 225 us
  Pallas kernels  219 us (96%)
  local copies, waits for them, and re-layouts  4.06 us (2%)
    pallas_call x1, Pallas kernels, fused(): pl.pallas_call(kernel, out_shape=jax.ShapeDtypeStruct((slots, piece, widt...  219 us

profile of v18, /device:TPU:69, one launch (start us, length us, event | category | flops | bytes accessed | tf_op | source)
XLA Modules:
  0.0 225.4 jit_solution(329973125325118248)
XLA Ops:
  0.0 0.7 compare_select_fusion
  0.7 0.8 copy.4
  1.5 1.0 scatter_custom_fusion
  2.5 0.1 copy.5
  2.6 0.1 reshape.3
  2.7 0.6 fusion.4.picked_ref
  3.3 0.6 and_select_fusion
  3.9 219.4 %shard_map.37 = f32[12,32,512]{2,1,0:T(8,128)} custom-call(s32[12]{0:T(128)} %get-tuple-element.6.holder_ref, s32[12]{0:T(128)} %get-tuple-element.5.rowblk_ref, s32[16]{0:T(128)} %fusion.4.picked_ref, bf16[512,2048]{1,0:T(8,128)(2,1)} %act_hbm.1), custom_call_target="tpu_custom_call" | custom-call | tf_op jit(solution)/shard_map/pallas_call | solution.py:216
  223.3 2.1 copy.7
  (1 shorter events, 0.0 us)

commit v19 on v18

--- a/solution.py
+++ b/solution.py
@@ -71,7 +71,7 @@
         return copies
 
     def reduce_last(c):
-        h = (slots * 5) // 12
+        h = (slots * 7) // 12
         cols = pl.ds(c * w, w)
         cp0 = pltpu.make_async_remote_copy(
             src_ref=gbuf.at[1 - core], dst_ref=st0.at[c], send_sem=send0.at[c],
@@ -242,9 +242,9 @@
             pltpu.SemaphoreType.DMA((CHUNKS, n_y)),
             pltpu.SemaphoreType.DMA((CHUNKS,)),
             pltpu.SemaphoreType.DMA((CHUNKS,)),
-            pltpu.VMEM((n_y, slots - (slots * 5) // 12, piece, w), jnp.float32),
-            pltpu.VMEM((n_y, slots - (slots * 5) // 12, piece, w), jnp.float32),
-            pltpu.VMEM((n_y, slots - (slots * 5) // 12, piece, w), jnp.float32),
+            pltpu.VMEM((n_y, slots - (slots * 7) // 12, piece, w), jnp.float32),
+            pltpu.VMEM((n_y, slots - (slots * 7) // 12, piece, w), jnp.float32),
+            pltpu.VMEM((n_y, slots - (slots * 7) // 12, piece, w), jnp.float32),
             pltpu.SemaphoreType.DMA((2,)),
             pltpu.SemaphoreType.DMA((n_y,)),
             pltpu.SemaphoreType.DMA((n_y,)),

time: 228 us -> 225 us (0.987)
    pallas_call x1, Pallas kernels: 219 us -> 217 us  [fused(): pl.pallas_call(kernel, out_shape=jax.ShapeDtypeStruct((slots, piece, widt...]
where the time goes in v19:
time: 225 us; the launch traced here: 223 us
  Pallas kernels  217 us (96%)
  local copies, waits for them, and re-layouts  4.06 us (2%)
    pallas_call x1, Pallas kernels, fused(): pl.pallas_call(kernel, out_shape=jax.ShapeDtypeStruct((slots, piece, widt...  217 us

profile of v19, /device:TPU:69, one launch (start us, length us, event | category | flops | bytes accessed | tf_op | source)
XLA Modules:
  0.0 222.6 jit_solution(347590879775426310)
XLA Ops:
  0.0 0.7 compare_select_fusion
  0.7 0.8 copy.4
  1.5 1.0 scatter_custom_fusion
  2.5 0.1 copy.5
  2.6 0.1 reshape.3
  2.7 0.6 fusion.4.picked_ref
  3.3 0.6 and_select_fusion
  3.9 216.7 %shard_map.37 = f32[12,32,512]{2,1,0:T(8,128)} custom-call(s32[12]{0:T(128)} %get-tuple-element.6.holder_ref, s32[12]{0:T(128)} %get-tuple-element.5.rowblk_ref, s32[16]{0:T(128)} %fusion.4.picked_ref, bf16[512,2048]{1,0:T(8,128)(2,1)} %act_hbm.1), custom_call_target="tpu_custom_call" | custom-call | tf_op jit(solution)/shard_map/pallas_call | solution.py:216
  220.6 2.1 copy.7
  (1 shorter events, 0.0 us)

commit v20 on v19

--- a/solution.py
+++ b/solution.py
@@ -128,15 +128,15 @@
         out_ref[:h, :, cols] = s2buf[x, :h] + st2[c, :h]
 
     in_flight = []
-    for c in range(min(2, chunks)):
+    for c in range(min(3, chunks)):
         in_flight.append(feat_copies(c))
         for cp in in_flight[-1]:
             cp.start()
     for c in range(chunks):
         for cp in in_flight[c]:
             cp.wait()
-        if c + 2 < chunks:
-            in_flight.append(feat_copies(c + 2))
+        if c + 3 < chunks:
+            in_flight.append(feat_copies(c + 3))
             for cp in in_flight[-1]:
                 cp.start()
 

time: 225 us -> 225 us (level)
  no operation moved by 1% of the time
where the time goes in v20:
time: 225 us; the launch traced here: 223 us
  Pallas kernels  217 us (96%)
  local copies, waits for them, and re-layouts  4.06 us (2%)
    pallas_call x1, Pallas kernels, fused(): pl.pallas_call(kernel, out_shape=jax.ShapeDtypeStruct((slots, piece, widt...  217 us

profile of v20, /device:TPU:69, one launch (start us, length us, event | category | flops | bytes accessed | tf_op | source)
XLA Modules:
  0.0 222.6 jit_solution(1527463597886346520)
XLA Ops:
  0.0 0.7 compare_select_fusion
  0.7 0.8 copy.4
  1.5 1.0 scatter_custom_fusion
  2.5 0.1 copy.5
  2.6 0.1 reshape.3
  2.7 0.6 fusion.4.picked_ref
  3.3 0.6 and_select_fusion
  3.9 216.7 %shard_map.37 = f32[12,32,512]{2,1,0:T(8,128)} custom-call(s32[12]{0:T(128)} %get-tuple-element.6.holder_ref, s32[12]{0:T(128)} %get-tuple-element.5.rowblk_ref, s32[16]{0:T(128)} %fusion.4.picked_ref, bf16[512,2048]{1,0:T(8,128)(2,1)} %act_hbm.1), custom_call_target="tpu_custom_call" | custom-call | tf_op jit(solution)/shard_map/pallas_call | solution.py:216
  220.6 2.1 copy.7
  (1 shorter events, 0.0 us)

commit v21 on v15

--- a/solution.py
+++ b/solution.py
@@ -58,7 +58,7 @@
         cols = pl.ds(c * w, w)
         local = pltpu.make_async_copy(send_ref.at[me, :, cols], recv[c].at[me], flocal.at[c])
         copies = [local]
-        for k in range(1, n_feat):
+        for k in sorted(range(1, n_feat), key=lambda k: min(k, n_feat - k)):
             peer = lax.rem(me + k, n_feat)
             copies.append(pltpu.make_async_remote_copy(
                 src_ref=send_ref.at[peer, :, cols],
@@ -70,8 +70,8 @@
             ))
         return copies
 
-    def reduce_last(c):
-        h = slots // 2
+    def reduce_last(c, gram_one):
+        h = (slots * 7) // 12
         cols = pl.ds(c * w, w)
         cp0a = pltpu.make_async_remote_copy(
             src_ref=gbuf.at[1 - core, :, :, pl.ds(0, h)], dst_ref=st0.at[c, :, :, pl.ds(0, h)],
@@ -82,7 +82,9 @@
             dst_ref=st0.at[c, :, :, pl.ds(h, slots - h)],
             send_sem=bsem.at[2], recv_sem=bsem.at[3], device_id={"tok": core_peer}, device_id_type=MESH,
         )
+        lax.fori_loop(0, h, gram_one, 0)
         cp0a.start()
+        lax.fori_loop(h, slots, gram_one, 0)
         cp0b.start()
         cp0a.wait()
         s1buf[:, :, :h] = gbuf[core, :, :, :h] + st0[c, :, :, :h]
@@ -161,11 +163,11 @@
                         gbuf[cc, yy, xx, k] = g[r0:r0 + piece, :]
             return carry
 
+        if c == chunks - 1 and slots > 1:
+            reduce_last(c, gram_one)
+            continue
+
         lax.fori_loop(0, slots, gram_one, 0)
-
-        if c == chunks - 1 and slots > 1:
-            reduce_last(c)
-            continue
 
         cp0 = pltpu.make_async_remote_copy(
             src_ref=gbuf.at[1 - core],
@@ -250,9 +252,9 @@
             pltpu.SemaphoreType.DMA((CHUNKS, n_y)),
             pltpu.SemaphoreType.DMA((CHUNKS,)),
             pltpu.SemaphoreType.DMA((CHUNKS,)),
-            pltpu.VMEM((n_y, slots - slots // 2, piece, w), jnp.float32),
-            pltpu.VMEM((n_y, slots - slots // 2, piece, w), jnp.float32),
-            pltpu.VMEM((n_y, slots - slots // 2, piece, w), jnp.float32),
+            pltpu.VMEM((n_y, slots - (slots * 7) // 12, piece, w), jnp.float32),
+            pltpu.VMEM((n_y, slots - (slots * 7) // 12, piece, w), jnp.float32),
+            pltpu.VMEM((n_y, slots - (slots * 7) // 12, piece, w), jnp.float32),
             pltpu.SemaphoreType.DMA((4,)),
             pltpu.SemaphoreType.DMA((n_y,)),
             pltpu.SemaphoreType.DMA((n_y,)),

time: 228 us -> 223 us (0.978)
  Pallas kernels: 220 us -> 214 us
    pallas_call x1, Pallas kernels: 220 us -> 214 us  [fused(): pl.pallas_call(kernel, out_shape=jax.ShapeDtypeStruct((slots, piece, widt...]
where the time goes in v21:
time: 223 us; the launch traced here: 220 us
  Pallas kernels  214 us (96%)
  local copies, waits for them, and re-layouts  4.06 us (2%)
    pallas_call x1, Pallas kernels, fused(): pl.pallas_call(kernel, out_shape=jax.ShapeDtypeStruct((slots, piece, widt...  214 us

profile of v21, /device:TPU:69, one launch (start us, length us, event | category | flops | bytes accessed | tf_op | source)
XLA Modules:
  0.0 220.1 jit_solution(15327639556845617925)
XLA Ops:
  0.0 0.7 compare_select_fusion
  0.7 0.8 copy.4
  1.5 1.0 scatter_custom_fusion
  2.5 0.1 copy.5
  2.6 0.1 reshape.3
  2.7 0.6 fusion.4.picked_ref
  3.3 0.6 and_select_fusion
  3.9 214.1 %shard_map.37 = f32[12,32,512]{2,1,0:T(8,128)} custom-call(s32[12]{0:T(128)} %get-tuple-element.6.holder_ref, s32[12]{0:T(128)} %get-tuple-element.5.rowblk_ref, s32[16]{0:T(128)} %fusion.4.picked_ref, bf16[512,2048]{1,0:T(8,128)(2,1)} %act_hbm.1), custom_call_target="tpu_custom_call" | custom-call | tf_op jit(solution)/shard_map/pallas_call | solution.py:226
  218.1 2.1 copy.7
  (1 shorter events, 0.0 us)

commit v22 on v21

--- a/solution.py
+++ b/solution.py
@@ -71,7 +71,7 @@
         return copies
 
     def reduce_last(c, gram_one):
-        h = (slots * 7) // 12
+        h = (slots * 8) // 12
         cols = pl.ds(c * w, w)
         cp0a = pltpu.make_async_remote_copy(
             src_ref=gbuf.at[1 - core, :, :, pl.ds(0, h)], dst_ref=st0.at[c, :, :, pl.ds(0, h)],
@@ -252,9 +252,9 @@
             pltpu.SemaphoreType.DMA((CHUNKS, n_y)),
             pltpu.SemaphoreType.DMA((CHUNKS,)),
             pltpu.SemaphoreType.DMA((CHUNKS,)),
-            pltpu.VMEM((n_y, slots - (slots * 7) // 12, piece, w), jnp.float32),
-            pltpu.VMEM((n_y, slots - (slots * 7) // 12, piece, w), jnp.float32),
-            pltpu.VMEM((n_y, slots - (slots * 7) // 12, piece, w), jnp.float32),
+            pltpu.VMEM((n_y, slots - (slots * 8) // 12, piece, w), jnp.float32),
+            pltpu.VMEM((n_y, slots - (slots * 8) // 12, piece, w), jnp.float32),
+            pltpu.VMEM((n_y, slots - (slots * 8) // 12, piece, w), jnp.float32),
             pltpu.SemaphoreType.DMA((4,)),
             pltpu.SemaphoreType.DMA((n_y,)),
             pltpu.SemaphoreType.DMA((n_y,)),

time: 223 us -> 225 us (level)
  no operation moved by 1% of the time
where the time goes in v22:
time: 225 us; the launch traced here: 222 us
  Pallas kernels  216 us (96%)
  local copies, waits for them, and re-layouts  4.06 us (2%)
    pallas_call x1, Pallas kernels, fused(): pl.pallas_call(kernel, out_shape=jax.ShapeDtypeStruct((slots, piece, widt...  216 us

profile of v22, /device:TPU:69, one launch (start us, length us, event | category | flops | bytes accessed | tf_op | source)
XLA Modules:
  0.0 222.2 jit_solution(13285550728545703430)
XLA Ops:
  0.0 0.7 compare_select_fusion
  0.7 0.8 copy.4
  1.5 1.0 scatter_custom_fusion
  2.5 0.1 copy.5
  2.6 0.1 reshape.3
  2.7 0.6 fusion.4.picked_ref
  3.3 0.6 and_select_fusion
  3.9 216.2 %shard_map.37 = f32[12,32,512]{2,1,0:T(8,128)} custom-call(s32[12]{0:T(128)} %get-tuple-element.6.holder_ref, s32[12]{0:T(128)} %get-tuple-element.5.rowblk_ref, s32[16]{0:T(128)} %fusion.4.picked_ref, bf16[512,2048]{1,0:T(8,128)(2,1)} %act_hbm.1), custom_call_target="tpu_custom_call" | custom-call | tf_op jit(solution)/shard_map/pallas_call | solution.py:226
  220.1 2.1 copy.7
  (1 shorter events, 0.0 us)

commit v23 on v22

--- a/solution.py
+++ b/solution.py
@@ -71,7 +71,7 @@
         return copies
 
     def reduce_last(c, gram_one):
-        h = (slots * 8) // 12
+        h = slots // 2
         cols = pl.ds(c * w, w)
         cp0a = pltpu.make_async_remote_copy(
             src_ref=gbuf.at[1 - core, :, :, pl.ds(0, h)], dst_ref=st0.at[c, :, :, pl.ds(0, h)],
@@ -252,9 +252,9 @@
             pltpu.SemaphoreType.DMA((CHUNKS, n_y)),
             pltpu.SemaphoreType.DMA((CHUNKS,)),
             pltpu.SemaphoreType.DMA((CHUNKS,)),
-            pltpu.VMEM((n_y, slots - (slots * 8) // 12, piece, w), jnp.float32),
-            pltpu.VMEM((n_y, slots - (slots * 8) // 12, piece, w), jnp.float32),
-            pltpu.VMEM((n_y, slots - (slots * 8) // 12, piece, w), jnp.float32),
+            pltpu.VMEM((n_y, slots - slots // 2, piece, w), jnp.float32),
+            pltpu.VMEM((n_y, slots - slots // 2, piece, w), jnp.float32),
+            pltpu.VMEM((n_y, slots - slots // 2, piece, w), jnp.float32),
             pltpu.SemaphoreType.DMA((4,)),
             pltpu.SemaphoreType.DMA((n_y,)),
             pltpu.SemaphoreType.DMA((n_y,)),

time: 225 us -> 225 us (level)
  no operation moved by 1% of the time
where the time goes in v23:
time: 225 us; the launch traced here: 222 us
  Pallas kernels  216 us (96%)
  local copies, waits for them, and re-layouts  4.06 us (2%)
    pallas_call x1, Pallas kernels, fused(): pl.pallas_call(kernel, out_shape=jax.ShapeDtypeStruct((slots, piece, widt...  216 us

profile of v23, /device:TPU:69, one launch (start us, length us, event | category | flops | bytes accessed | tf_op | source)
XLA Modules:
  0.0 222.1 jit_solution(307459747976066809)
XLA Ops:
  0.0 0.7 compare_select_fusion
  0.7 0.8 copy.4
  1.5 1.0 scatter_custom_fusion
  2.5 0.1 copy.5
  2.6 0.1 reshape.3
  2.7 0.6 fusion.4.picked_ref
  3.3 0.6 and_select_fusion
  3.9 216.1 %shard_map.37 = f32[12,32,512]{2,1,0:T(8,128)} custom-call(s32[12]{0:T(128)} %get-tuple-element.6.holder_ref, s32[12]{0:T(128)} %get-tuple-element.5.rowblk_ref, s32[16]{0:T(128)} %fusion.4.picked_ref, bf16[512,2048]{1,0:T(8,128)(2,1)} %act_hbm.1), custom_call_target="tpu_custom_call" | custom-call | tf_op jit(solution)/shard_map/pallas_call | solution.py:226
  220.0 2.1 copy.7
  (1 shorter events, 0.0 us)

commit v24 on v21

--- a/solution.py
+++ b/solution.py
@@ -89,7 +89,7 @@
         cp0a.wait()
         s1buf[:, :, :h] = gbuf[core, :, :, :h] + st0[c, :, :, :h]
         a_y = []
-        for o in range(1, n_y):
+        for o in sorted(range(1, n_y), key=lambda o: min(o, n_y - o)):
             dy = lax.rem(y + o, n_y)
             cp = pltpu.make_async_remote_copy(
                 src_ref=s1buf.at[dy, :, pl.ds(0, h)], dst_ref=st1.at[c, y, :, pl.ds(0, h)],
@@ -108,7 +108,7 @@
         b_x.wait()
         bsum[...] = s1buf[:, x, h:] + bxbuf[...]
         b_y = []
-        for o in range(1, n_y):
+        for o in sorted(range(1, n_y), key=lambda o: min(o, n_y - o)):
             dy = lax.rem(y + o, n_y)
             cp = pltpu.make_async_remote_copy(
                 src_ref=bsum.at[dy], dst_ref=bybuf.at[y],
@@ -182,7 +182,7 @@
         s1buf[...] = gbuf[core] + st0[c]
 
         copies1 = []
-        for o in range(1, n_y):
+        for o in sorted(range(1, n_y), key=lambda o: min(o, n_y - o)):
             dy = lax.rem(y + o, n_y)
             cp = pltpu.make_async_remote_copy(
                 src_ref=s1buf.at[dy],

time: 223 us -> 223 us (level)
  no operation moved by 1% of the time
where the time goes in v24:
time: 223 us; the launch traced here: 220 us
  Pallas kernels  214 us (96%)
  local copies, waits for them, and re-layouts  4.06 us (2%)
    pallas_call x1, Pallas kernels, fused(): pl.pallas_call(kernel, out_shape=jax.ShapeDtypeStruct((slots, piece, widt...  214 us

profile of v24, /device:TPU:69, one launch (start us, length us, event | category | flops | bytes accessed | tf_op | source)
XLA Modules:
  0.0 220.1 jit_solution(18337162895032833631)
XLA Ops:
  0.0 0.7 compare_select_fusion
  0.7 0.8 copy.4
  1.5 1.0 scatter_custom_fusion
  2.5 0.1 copy.5
  2.6 0.1 reshape.3
  2.7 0.6 fusion.4.picked_ref
  3.3 0.6 and_select_fusion
  3.9 214.1 %shard_map.37 = f32[12,32,512]{2,1,0:T(8,128)} custom-call(s32[12]{0:T(128)} %get-tuple-element.6.holder_ref, s32[12]{0:T(128)} %get-tuple-element.5.rowblk_ref, s32[16]{0:T(128)} %fusion.4.picked_ref, bf16[512,2048]{1,0:T(8,128)(2,1)} %act_hbm.1), custom_call_target="tpu_custom_call" | custom-call | tf_op jit(solution)/shard_map/pallas_call | solution.py:226
  218.1 2.1 copy.7
  (1 shorter events, 0.0 us)

commit v25 on v21

--- a/solution.py
+++ b/solution.py
@@ -57,7 +57,7 @@
     def feat_copies(c):
         cols = pl.ds(c * w, w)
         local = pltpu.make_async_copy(send_ref.at[me, :, cols], recv[c].at[me], flocal.at[c])
-        copies = [local]
+        copies = []
         for k in sorted(range(1, n_feat), key=lambda k: min(k, n_feat - k)):
             peer = lax.rem(me + k, n_feat)
             copies.append(pltpu.make_async_remote_copy(
@@ -68,6 +68,7 @@
                 device_id={"feat": peer},
                 device_id_type=MESH,
             ))
+        copies.append(local)
         return copies
 
     def reduce_last(c, gram_one):

time: 223 us -> 223 us (level)
  no operation moved by 1% of the time
where the time goes in v25:
time: 223 us; the launch traced here: 220 us
  Pallas kernels  214 us (96%)
  local copies, waits for them, and re-layouts  4.06 us (2%)
    pallas_call x1, Pallas kernels, fused(): pl.pallas_call(kernel, out_shape=jax.ShapeDtypeStruct((slots, piece, widt...  214 us

profile of v25, /device:TPU:69, one launch (start us, length us, event | category | flops | bytes accessed | tf_op | source)
XLA Modules:
  0.0 220.1 jit_solution(17133390938967346162)
XLA Ops:
  0.0 0.7 compare_select_fusion
  0.7 0.8 copy.4
  1.5 1.0 scatter_custom_fusion
  2.5 0.1 copy.5
  2.6 0.1 reshape.3
  2.7 0.6 fusion.4.picked_ref
  3.3 0.6 and_select_fusion
  3.9 214.1 %shard_map.37 = f32[12,32,512]{2,1,0:T(8,128)} custom-call(s32[12]{0:T(128)} %get-tuple-element.6.holder_ref, s32[12]{0:T(128)} %get-tuple-element.5.rowblk_ref, s32[16]{0:T(128)} %fusion.4.picked_ref, bf16[512,2048]{1,0:T(8,128)(2,1)} %act_hbm.1), custom_call_target="tpu_custom_call" | custom-call | tf_op jit(solution)/shard_map/pallas_call | solution.py:227
  218.1 2.1 copy.7
  (1 shorter events, 0.0 us)

commit v26 on v21

--- a/solution.py
+++ b/solution.py
@@ -58,7 +58,7 @@
         cols = pl.ds(c * w, w)
         local = pltpu.make_async_copy(send_ref.at[me, :, cols], recv[c].at[me], flocal.at[c])
         copies = [local]
-        for k in sorted(range(1, n_feat), key=lambda k: min(k, n_feat - k)):
+        for k in sorted(range(1, n_feat), key=lambda k: min(k, n_feat - k) + 2 * (k % 2)):
             peer = lax.rem(me + k, n_feat)
             copies.append(pltpu.make_async_remote_copy(
                 src_ref=send_ref.at[peer, :, cols],

time: 223 us -> 224 us (level)
  no operation moved by 1% of the time
where the time goes in v26:
time: 224 us; the launch traced here: 221 us
  Pallas kernels  215 us (96%)
  local copies, waits for them, and re-layouts  4.06 us (2%)
    pallas_call x1, Pallas kernels, fused(): pl.pallas_call(kernel, out_shape=jax.ShapeDtypeStruct((slots, piece, widt...  215 us

profile of v26, /device:TPU:69, one launch (start us, length us, event | category | flops | bytes accessed | tf_op | source)
XLA Modules:
  0.0 221.4 jit_solution(17404537559624971483)
XLA Ops:
  0.0 0.7 compare_select_fusion
  0.7 0.8 copy.4
  1.5 1.0 scatter_custom_fusion
  2.5 0.1 copy.5
  2.6 0.1 reshape.3
  2.7 0.6 fusion.4.picked_ref
  3.3 0.6 and_select_fusion
  3.9 215.5 %shard_map.37 = f32[12,32,512]{2,1,0:T(8,128)} custom-call(s32[12]{0:T(128)} %get-tuple-element.6.holder_ref, s32[12]{0:T(128)} %get-tuple-element.5.rowblk_ref, s32[16]{0:T(128)} %fusion.4.picked_ref, bf16[512,2048]{1,0:T(8,128)(2,1)} %act_hbm.1), custom_call_target="tpu_custom_call" | custom-call | tf_op jit(solution)/shard_map/pallas_call | solution.py:226
  219.4 2.1 copy.7
  (1 shorter events, 0.0 us)
